TPU v7x, 128 devices: a whole 4x4x4 slice. The times are simulated.
128 devices in a mesh: seq: 8 (over z, y_hi), dp: 16 (over y_lo, x, core).
Axes of the slice: x: 4, y: 4 (y_hi: 2, y_lo: 2; y = y_hi * 2 + y_lo), z: 4, core: 2. Of those that a mesh axis runs over, the one named last changes fastest.
Arguments:
- queries: bfloat16 [16, 2048, 1024], P('dp', 'seq'), may hold values from -24 to 24
- keys: bfloat16 [16, 2048, 1024], P('dp', 'seq'), may hold values from -4 to 4
- values: bfloat16 [16, 2048, 1024], P('dp', 'seq'), may hold values from -6 to 6
- out_proj: bfloat16 [1024, 2048], P('dp'), may hold values from -0.1875 to 0.1875
- grad_out: bfloat16 [16, 2048, 2048], P('dp', 'seq'), may hold values from -24 to 24
Outputs:
- grad_qkv: bfloat16 [16, 2048, 3072], P('dp', 'seq')
- grad_weight: float32 [1024, 2048], P('dp')
All inputs are finite; a program needn't handle non-finite values.
Results may differ from a plain program's by a relative error of at most 0.0058.
Values may be sent and summed in bfloat16 or wider, within the bound.
A program may use at most 64 MiB of HBM per device.

v0:
```python
from functools import partial

import jax
import jax.numpy as jnp
from jax import lax
from jax.sharding import PartitionSpec as P

HEAD_DIM = 64


def attend_block(totals, current, keys_head, values_head, scaling):
    sum_k, sum_v = totals
    query_rows, grad_rows = current
    scores = (
        jnp.einsum("qhd,khd->hqk", query_rows, keys_head, preferred_element_type=jnp.float32)
        * scaling
    )
    row_max = jnp.max(scores, axis=2, keepdims=True)
    exp_scores = jnp.exp(scores - row_max)
    probs = exp_scores / jnp.sum(exp_scores, axis=2, keepdims=True)
    probs_low = probs.astype(jnp.bfloat16)
    attn_rows = jnp.einsum(
        "hqk,khd->qhd", probs_low, values_head, preferred_element_type=jnp.float32
    ).astype(jnp.bfloat16)
    grad_prob = jnp.einsum(
        "qhd,khd->hqk", grad_rows, values_head, preferred_element_type=jnp.float32
    )
    row_dot = jnp.sum(probs * grad_prob, axis=2, keepdims=True)
    grad_score = (scaling * probs * (grad_prob - row_dot)).astype(jnp.bfloat16)
    grad_q = jnp.einsum(
        "hqk,khd->qhd", grad_score, keys_head, preferred_element_type=jnp.float32
    ).astype(jnp.bfloat16)
    sum_k = sum_k + jnp.einsum(
        "hqk,qhd->khd", grad_score, query_rows, preferred_element_type=jnp.float32
    )
    sum_v = sum_v + jnp.einsum(
        "hqk,qhd->khd", probs_low, grad_rows, preferred_element_type=jnp.float32
    )
    return ((sum_k, sum_v), (attn_rows, grad_q))


def on_device(queries, keys, values, out_proj, grad_out):
    grad_tokens = grad_out[0]
    grad_attn = lax.dot_general(
        grad_tokens,
        lax.all_gather(out_proj, "dp", axis=0, tiled=True),
        (((1,), (1,)), ((), ())),
        preferred_element_type=jnp.float32,
    ).astype(jnp.bfloat16)
    head_q, head_k, head_v, head_g = (
        lax.all_to_all(queries[0], "seq", split_axis=1, concat_axis=0, tiled=True),
        lax.all_to_all(keys[0], "seq", split_axis=1, concat_axis=0, tiled=True),
        lax.all_to_all(values[0], "seq", split_axis=1, concat_axis=0, tiled=True),
        lax.all_to_all(grad_attn, "seq", split_axis=1, concat_axis=0, tiled=True),
    )
    length, columns = head_q.shape
    local_heads = columns // HEAD_DIM
    block_rows = min(512, length)
    blocks = length // block_rows
    keys_head = head_k.reshape(length, local_heads, HEAD_DIM)
    values_head = head_v.reshape(length, local_heads, HEAD_DIM)
    query_blocks = head_q.reshape(blocks, block_rows, local_heads, HEAD_DIM)
    grad_blocks = head_g.reshape(blocks, block_rows, local_heads, HEAD_DIM)
    zeros_head = jnp.zeros((length, local_heads, HEAD_DIM), jnp.float32)
    step_fn = partial(
        attend_block, keys_head=keys_head, values_head=values_head, scaling=HEAD_DIM ** (-0.5)
    )
    (sum_k, sum_v), (attn_blocks, grad_q_blocks) = lax.scan(
        step_fn, (zeros_head, zeros_head), (query_blocks, grad_blocks)
    )
    head_out = attn_blocks.reshape(length, columns)
    head_dq = grad_q_blocks.reshape(length, columns)
    head_dk = sum_k.astype(jnp.bfloat16).reshape(length, columns)
    head_dv = sum_v.astype(jnp.bfloat16).reshape(length, columns)
    token_out, token_dq, token_dk, token_dv = (
        lax.all_to_all(head_out, "seq", split_axis=0, concat_axis=1, tiled=True),
        lax.all_to_all(head_dq, "seq", split_axis=0, concat_axis=1, tiled=True),
        lax.all_to_all(head_dk, "seq", split_axis=0, concat_axis=1, tiled=True),
        lax.all_to_all(head_dv, "seq", split_axis=0, concat_axis=1, tiled=True),
    )
    grad_qkv = jnp.concatenate([token_dq, token_dk, token_dv], axis=1)[None]
    share = lax.psum_scatter(
        lax.dot_general(
            token_out, grad_tokens, (((0,), (0,)), ((), ())), preferred_element_type=jnp.float32
        ),
        "dp",
        scatter_dimension=0,
        tiled=True,
    )
    grad_weight = lax.psum(share, "seq")
    return (grad_qkv, grad_weight)


def solution(mesh):
    return jax.shard_map(
        on_device,
        mesh=mesh,
        in_specs=(
            P("dp", "seq", None),
            P("dp", "seq", None),
            P("dp", "seq", None),
            P("dp", None),
            P("dp", "seq", None),
        ),
        out_specs=(P("dp", "seq", None), P("dp", None)),
        check_vma=False,
    )
```

profile of v0, /device:TPU:1, one launch (start us, length us, event | category | flops | bytes accessed | tf_op | source)
XLA Modules:
  0.0 385.2 jit_solution(15511967211419384180)
XLA Ops:
  10.0 8.5 %all-to-all-start = ((bf16[256,8,128]{0,2,1:T(8,128)(2,1)}), bf16[256,8,128]{0,2,1:T(8,128)(2,1)S(1)}, u32[]{:S(2)}, u32[]{:S(2)}) async-start(bf16[256,8,128]{0,2,1:T(8,128)(2,1)} %bitcast), calls=%async_computation | async-start | bytes 1048576 | tf_op jit(solution)/shard_map/all_to_all | solution.py:51
  20.5 9.4 %all-to-all-done = bf16[256,8,128]{0,2,1:T(8,128)(2,1)S(1)} async-done(((bf16[256,8,128]{0,2,1:T(8,128)(2,1)}), bf16[256,8,128]{0,2,1:T(8,128)(2,1)S(1)}, u32[]{:S(2)}, u32[]{:S(2)}) %all-to-all-start) | async-done | bytes 524320 | tf_op jit(solution)/shard_map/all_to_all | solution.py:51
  29.9 3.5 all-to-all-start.1
  33.4 2.0 copy.56
  35.5 13.4 %all-to-all-done.1 = bf16[256,8,128]{0,2,1:T(8,128)(2,1)S(1)} async-done(((bf16[256,8,128]{0,2,1:T(8,128)(2,1)}), bf16[256,8,128]{0,2,1:T(8,128)(2,1)S(1)}, u32[]{:S(2)}, u32[]{:S(2)}) %all-to-all-start.1) | async-done | bytes 524320 | tf_op jit(solution)/shard_map/all_to_all | solution.py:52
  48.8 3.5 all-to-all-start.3
  53.4 3.5 convolution_convert_fusion.1
  57.9 3.4 all-to-all-done.3
  61.3 4.1 %all-to-all-start.2 = ((bf16[256,8,128]{0,2,1:T(8,128)(2,1)}), bf16[256,8,128]{0,2,1:T(8,128)(2,1)}, u32[]{:S(2)}, u32[]{:S(2)}) async-start(bf16[256,8,128]{0,2,1:T(8,128)(2,1)} %bitcast.5), calls=%async_computation.2 | async-start | bytes 1048576 | tf_op jit(solution)/shard_map/all_to_all | solution.py:54
  66.8 2.2 reshape.58
  72.5 2.1 copy.57
  74.7 2.1 reshape.61
  76.8 2.1 copy.55
  78.9 2.2 reshape.60
  83.0 108.8 %while.17 = (s32[]{:T(128)}, f32[2048,2,64]{0,2,1:T(8,128)S(1)}, f32[2048,2,64]{0,2,1:T(8,128)}, bf16[4,512,2,64]{1,3,2,0:T(8,128)(2,1)}, bf16[4,512,2,64]{1,3,2...) while((s32[]{:T(128)}, f32[2048,2,64]{0,2,1:T(8,128)S(1)}, ...), condition=%wide.region_4.5_spmd.clone, body=%wide.region_0.4_spmd.clone.sunk | while | flops 1643250688 | bytes 156006672 | solution.py:68
  83.0 4.9 %fusion.93 = (f32[2,512]{1,0:T(2,128)S(1)}, f32[2,512,2048]{2,1,0:T(8,128)}) fusion(bf16[2048,2,64]{0,2,1:T(8,128)(2,1)S(1)} %get-tuple-element.241, bf16[4,512,2,64]{1,3,2,0:T(8,128)(2,1)S(1)} %get-tuple-element.240, s32[]{:T(128)} %get-tuple-element.224), kind=kOutput, calls=%fused_computation.45.clone.1 | convolution fusion | flops 274728960 | bytes 9048068 | tf_op jit(solution)/shard_map/while/body/eval_jaxpr/sub | solution.py:19
  88.0 5.2 %multiply_reduce_fusion.3 = (f32[2,512]{1,0:T(2,128)S(1)}, f32[2,512,2048]{2,1,0:T(8,128)S(1)}) fusion(f32[2,512,2048]{2,1,0:T(8,128)} %get-tuple-element.209, f32[2,512]{1,0:T(2,128)S(1)} %get-tuple-element.210, bf16[2048,2,64]{0,2,1:T(8,128)(2,1)} %get-tuple-element.243, bf16[4,512,2,64]{1,3,2,0:T(8,128)(2,1)} %get-tuple-element.242, ...), kind=kOutput, calls=%fused_computation.2.clone.1 | convolution fusion | flops 274725888 | bytes 17441280 | tf_op jit(solution)/shard_map/while/body/eval_jaxpr/qhd,khd->hqk/dot_general | solution.py:25
  93.9 2.9 multiply_convert_fusion.2
  96.9 3.3 fusion.94
  102.4 5.5 %fusion.95 = f32[2048,2,64]{0,2,1:T(8,128)} fusion(f32[2048,2,64]{0,2,1:T(8,128)} %get-tuple-element.226, pred[]{:T(512)S(6)} %compare.3, bf16[4,512,2,64]{1,3,2,0:T(8,128)(2,1)} %get-tuple-element.242, s32[]{:T(128)} %get-tuple-element.224, f32[2,512,2048]{2,1,0:T(8,128)} %get-tuple-element.209, f32[2,512]{1,0:T(2,128)S(1)} %get-tuple-element.210), kind=kOutput, calls=%fused_computation.9.clone.1 | convolution fusion | flops 273154048 | bytes 10621441 | tf_op jit(solution)/shard_map/while/body/eval_jaxpr/hqk,qhd->khd/dot_general | solution.py:36
  107.9 2.1 fusion.96
  110.0 4.9 %fusion.93 = (f32[2,512]{1,0:T(2,128)S(1)}, f32[2,512,2048]{2,1,0:T(8,128)}) fusion(bf16[2048,2,64]{0,2,1:T(8,128)(2,1)S(1)} %get-tuple-element.241, bf16[4,512,2,64]{1,3,2,0:T(8,128)(2,1)S(1)} %get-tuple-element.240, s32[]{:T(128)} %get-tuple-element.224), kind=kOutput, calls=%fused_computation.45.clone.1 | convolution fusion | flops 274728960 | bytes 9048068 | tf_op jit(solution)/shard_map/while/body/eval_jaxpr/sub | solution.py:19
  115.0 5.2 %multiply_reduce_fusion.3 = (f32[2,512]{1,0:T(2,128)S(1)}, f32[2,512,2048]{2,1,0:T(8,128)S(1)}) fusion(f32[2,512,2048]{2,1,0:T(8,128)} %get-tuple-element.209, f32[2,512]{1,0:T(2,128)S(1)} %get-tuple-element.210, bf16[2048,2,64]{0,2,1:T(8,128)(2,1)} %get-tuple-element.243, bf16[4,512,2,64]{1,3,2,0:T(8,128)(2,1)} %get-tuple-element.242, ...), kind=kOutput, calls=%fused_computation.2.clone.1 | convolution fusion | flops 274725888 | bytes 17441280 | tf_op jit(solution)/shard_map/while/body/eval_jaxpr/qhd,khd->hqk/dot_general | solution.py:25
  120.9 2.9 multiply_convert_fusion.2
  123.9 3.3 fusion.94
  129.4 5.7 %fusion.95 = f32[2048,2,64]{0,2,1:T(8,128)} fusion(f32[2048,2,64]{0,2,1:T(8,128)} %get-tuple-element.226, pred[]{:T(512)S(6)} %compare.3, bf16[4,512,2,64]{1,3,2,0:T(8,128)(2,1)} %get-tuple-element.242, s32[]{:T(128)} %get-tuple-element.224, f32[2,512,2048]{2,1,0:T(8,128)} %get-tuple-element.209, f32[2,512]{1,0:T(2,128)S(1)} %get-tuple-element.210), kind=kOutput, calls=%fused_computation.9.clone.1 | convolution fusion | flops 273154048 | bytes 10621441 | tf_op jit(solution)/shard_map/while/body/eval_jaxpr/hqk,qhd->khd/dot_general | solution.py:36
  135.1 2.1 fusion.96
  137.3 4.9 %fusion.93 = (f32[2,512]{1,0:T(2,128)S(1)}, f32[2,512,2048]{2,1,0:T(8,128)}) fusion(bf16[2048,2,64]{0,2,1:T(8,128)(2,1)S(1)} %get-tuple-element.241, bf16[4,512,2,64]{1,3,2,0:T(8,128)(2,1)S(1)} %get-tuple-element.240, s32[]{:T(128)} %get-tuple-element.224), kind=kOutput, calls=%fused_computation.45.clone.1 | convolution fusion | flops 274728960 | bytes 9048068 | tf_op jit(solution)/shard_map/while/body/eval_jaxpr/sub | solution.py:19
  142.2 5.2 %multiply_reduce_fusion.3 = (f32[2,512]{1,0:T(2,128)S(1)}, f32[2,512,2048]{2,1,0:T(8,128)S(1)}) fusion(f32[2,512,2048]{2,1,0:T(8,128)} %get-tuple-element.209, f32[2,512]{1,0:T(2,128)S(1)} %get-tuple-element.210, bf16[2048,2,64]{0,2,1:T(8,128)(2,1)} %get-tuple-element.243, bf16[4,512,2,64]{1,3,2,0:T(8,128)(2,1)} %get-tuple-element.242, ...), kind=kOutput, calls=%fused_computation.2.clone.1 | convolution fusion | flops 274725888 | bytes 17441280 | tf_op jit(solution)/shard_map/while/body/eval_jaxpr/qhd,khd->hqk/dot_general | solution.py:25
  148.2 2.9 multiply_convert_fusion.2
  151.1 3.3 fusion.94
  156.6 5.7 %fusion.95 = f32[2048,2,64]{0,2,1:T(8,128)} fusion(f32[2048,2,64]{0,2,1:T(8,128)} %get-tuple-element.226, pred[]{:T(512)S(6)} %compare.3, bf16[4,512,2,64]{1,3,2,0:T(8,128)(2,1)} %get-tuple-element.242, s32[]{:T(128)} %get-tuple-element.224, f32[2,512,2048]{2,1,0:T(8,128)} %get-tuple-element.209, f32[2,512]{1,0:T(2,128)S(1)} %get-tuple-element.210), kind=kOutput, calls=%fused_computation.9.clone.1 | convolution fusion | flops 273154048 | bytes 10621441 | tf_op jit(solution)/shard_map/while/body/eval_jaxpr/hqk,qhd->khd/dot_general | solution.py:36
  162.4 2.1 fusion.96
  164.5 4.9 %fusion.93 = (f32[2,512]{1,0:T(2,128)S(1)}, f32[2,512,2048]{2,1,0:T(8,128)}) fusion(bf16[2048,2,64]{0,2,1:T(8,128)(2,1)S(1)} %get-tuple-element.241, bf16[4,512,2,64]{1,3,2,0:T(8,128)(2,1)S(1)} %get-tuple-element.240, s32[]{:T(128)} %get-tuple-element.224), kind=kOutput, calls=%fused_computation.45.clone.1 | convolution fusion | flops 274728960 | bytes 9048068 | tf_op jit(solution)/shard_map/while/body/eval_jaxpr/sub | solution.py:19
  169.5 5.2 %multiply_reduce_fusion.3 = (f32[2,512]{1,0:T(2,128)S(1)}, f32[2,512,2048]{2,1,0:T(8,128)S(1)}) fusion(f32[2,512,2048]{2,1,0:T(8,128)} %get-tuple-element.209, f32[2,512]{1,0:T(2,128)S(1)} %get-tuple-element.210, bf16[2048,2,64]{0,2,1:T(8,128)(2,1)} %get-tuple-element.243, bf16[4,512,2,64]{1,3,2,0:T(8,128)(2,1)} %get-tuple-element.242, ...), kind=kOutput, calls=%fused_computation.2.clone.1 | convolution fusion | flops 274725888 | bytes 17441280 | tf_op jit(solution)/shard_map/while/body/eval_jaxpr/qhd,khd->hqk/dot_general | solution.py:25
  175.4 2.9 multiply_convert_fusion.2
  178.4 3.3 fusion.94
  183.9 5.7 %fusion.95 = f32[2048,2,64]{0,2,1:T(8,128)} fusion(f32[2048,2,64]{0,2,1:T(8,128)} %get-tuple-element.226, pred[]{:T(512)S(6)} %compare.3, bf16[4,512,2,64]{1,3,2,0:T(8,128)(2,1)} %get-tuple-element.242, s32[]{:T(128)} %get-tuple-element.224, f32[2,512,2048]{2,1,0:T(8,128)} %get-tuple-element.209, f32[2,512]{1,0:T(2,128)S(1)} %get-tuple-element.210), kind=kOutput, calls=%fused_computation.9.clone.1 | convolution fusion | flops 273154048 | bytes 10621441 | tf_op jit(solution)/shard_map/while/body/eval_jaxpr/hqk,qhd->khd/dot_general | solution.py:36
  189.6 2.1 fusion.96
  193.5 15.2 %all_to_all.140 = bf16[8,256,128]{1,2,0:T(8,128)(2,1)S(1)} all-to-all(bf16[8,256,128]{1,2,0:T(8,128)(2,1)S(1)} %copy.65), channel_id=1, replica_groups=mesh['seq'=8,'dp'=16] {'seq'}, dimensions={0} | all-to-all | bytes 1048576 | tf_op jit(solution)/shard_map/all_to_all | solution.py:76
  208.6 4.5 %fusion.49 = f32[1024,2048]{1,0:T(8,128)} fusion(bf16[256,1024]{0,1:T(8,128)(2,1)S(1)} %bitcast.130, bf16[1,256,2048]{2,1,0:T(8,128)(2,1)S(1)} %copy-done), kind=kOutput, calls=%fused_computation.42 | convolution fusion | flops 1073741824 | bytes 9961472 | tf_op jit(solution)/shard_map/dot_general | solution.py:83
  214.7 3.5 all-to-all-start.4
  219.2 7.9 %all-to-all-done.4 = bf16[8,256,128]{1,2,0:T(8,128)(2,1)S(1)} async-done(((bf16[8,256,128]{1,2,0:T(8,128)(2,1)}), bf16[8,256,128]{1,2,0:T(8,128)(2,1)S(1)}, u32[]{:S(2)}, u32[]{:S(2)}) %all-to-all-start.4) | async-done | bytes 524320 | tf_op jit(solution)/shard_map/all_to_all | solution.py:77
  227.1 3.5 all-to-all-start.5
  233.0 17.6 %all-to-all-done.5 = bf16[8,256,128]{1,2,0:T(8,128)(2,1)S(1)} async-done(((bf16[8,256,128]{1,2,0:T(8,128)(2,1)}), bf16[8,256,128]{1,2,0:T(8,128)(2,1)S(1)}, u32[]{:S(2)}, u32[]{:S(2)}) %all-to-all-start.5) | async-done | bytes 524320 | tf_op jit(solution)/shard_map/all_to_all | solution.py:78
  250.5 3.5 all-to-all-start.6
  254.1 36.5 %reduce-scatter.2.cloned.1.call-done = f32[64,2048]{1,0:T(8,128)} async-done(((f32[1024,2048]{1,0:T(8,128)}), f32[64,2048]{1,0:T(8,128)}) %reduce-scatter.2.cloned.1.call-update) | async-done | bytes 524304 | tf_op jit(solution)/shard_map/reduce_scatter | solution.py:82
  294.5 82.3 %all-reduce.2.cloned.1.call-done = f32[64,2048]{1,0:T(8,128)} async-done(((f32[64,2048]{1,0:T(8,128)}), f32[64,2048]{1,0:T(8,128)}) %all-reduce.2.cloned.1.call-update) | async-done | bytes 524304 | tf_op jit(solution)/shard_map/psum | solution.py:90
  (94 shorter events, 37.9 us)
Async XLA Ops:
  7.2 46.2 %copy-start = (bf16[1,256,2048]{2,1,0:T(8,128)(2,1)S(1)}, bf16[1,256,2048]{2,1,0:T(8,128)(2,1)}, u32[]{:S(2)}) copy-start(bf16[1,256,2048]{2,1,0:T(8,128)(2,1)} %param.11) | copy-start | bytes 3145732
  7.2 46.2 %all-gather.2.cloned.1.call-start = ((), (), s32[]{:S(2)}) async-start(), calls=%async_computation.9 | async-start | bytes 4456448 | tf_op jit(solution)/shard_map/all_gather | solution.py:46
  10.0 19.9 %all-to-all-start = ((bf16[256,8,128]{0,2,1:T(8,128)(2,1)}), bf16[256,8,128]{0,2,1:T(8,128)(2,1)S(1)}, u32[]{:S(2)}, u32[]{:S(2)}) async-start(bf16[256,8,128]{0,2,1:T(8,128)(2,1)} %bitcast), calls=%async_computation | async-start | bytes 1048576 | tf_op jit(solution)/shard_map/all_to_all | solution.py:51
  29.9 18.9 %all-to-all-start.1 = ((bf16[256,8,128]{0,2,1:T(8,128)(2,1)}), bf16[256,8,128]{0,2,1:T(8,128)(2,1)S(1)}, u32[]{:S(2)}, u32[]{:S(2)}) async-start(bf16[256,8,128]{0,2,1:T(8,128)(2,1)} %bitcast.2), calls=%async_computation.1 | async-start | bytes 1048576 | tf_op jit(solution)/shard_map/all_to_all | solution.py:52
  48.8 12.5 %all-to-all-start.3 = ((bf16[256,8,128]{0,2,1:T(8,128)(2,1)}), bf16[256,8,128]{0,2,1:T(8,128)(2,1)S(1)}, u32[]{:S(2)}, u32[]{:S(2)}) async-start(bf16[256,8,128]{0,2,1:T(8,128)(2,1)} %bitcast.7), calls=%async_computation.3 | async-start | bytes 1048576 | tf_op jit(solution)/shard_map/all_to_all | solution.py:53
  61.3 4.2 %copy-start.3 = (bf16[256,8,128]{0,2,1:T(8,128)(2,1)}, bf16[256,8,128]{0,2,1:T(8,128)(2,1)S(1)}, u32[]{:S(2)}) copy-start(bf16[256,8,128]{0,2,1:T(8,128)(2,1)S(1)} %all-to-all-done.3) | copy-start | bytes 1572868
  61.3 15.5 %all-to-all-start.2 = ((bf16[256,8,128]{0,2,1:T(8,128)(2,1)}), bf16[256,8,128]{0,2,1:T(8,128)(2,1)}, u32[]{:S(2)}, u32[]{:S(2)}) async-start(bf16[256,8,128]{0,2,1:T(8,128)(2,1)} %bitcast.5), calls=%async_computation.2 | async-start | bytes 1048576 | tf_op jit(solution)/shard_map/all_to_all | solution.py:54
  65.5 225.1 %reduce-scatter.2.cloned.1.call-start = ((), (), s32[]{:S(2)}) async-start(), calls=%async_computation.10 | async-start | bytes 8912896 | tf_op jit(solution)/shard_map/reduce_scatter | solution.py:82
  88.0 6.0 %copy-start.2 = (f32[2,512,2048]{2,1,0:T(8,128)S(1)}, f32[2,512,2048]{2,1,0:T(8,128)}, u32[]{:S(2)}) copy-start(f32[2,512,2048]{2,1,0:T(8,128)} %get-tuple-element.209) | copy-start | bytes 25165828 | tf_op jit(solution)/shard_map/while
  96.9 3.4 copy-start.1
  100.3 7.6 %slice-start = ((s8[8388608]{0:T(1024)(128)(4,1)}), s8[4194304]{0:T(1024)(128)(4,1)S(1)}, s32[]{:S(2)}) async-start(s8[8388608]{0:T(1024)(128)(4,1)} %bitcast.128), calls=%async_computation.12 | async-start | bytes 8388608 | tf_op jit(solution)/shard_map/while
  102.4 5.5 %slice-start.1 = ((s8[8388608]{0:T(1024)(128)(4,1)}), s8[4194304]{0:T(1024)(128)(4,1)S(1)}, s32[]{:S(2)}) async-start(s8[8388608]{0:T(1024)(128)(4,1)} %bitcast.128), calls=%async_computation.13 | async-start | bytes 8388608 | tf_op jit(solution)/shard_map/while
  102.4 5.5 %copy-start.6 = (bf16[2048,2,64]{0,2,1:T(8,128)(2,1)S(1)}, bf16[2048,2,64]{0,2,1:T(8,128)(2,1)}, u32[]{:S(2)}) copy-start(bf16[2048,2,64]{0,2,1:T(8,128)(2,1)} %get-tuple-element.243) | copy-start | bytes 1572868 | tf_op jit(solution)/shard_map/while
  115.0 6.0 %copy-start.2 = (f32[2,512,2048]{2,1,0:T(8,128)S(1)}, f32[2,512,2048]{2,1,0:T(8,128)}, u32[]{:S(2)}) copy-start(f32[2,512,2048]{2,1,0:T(8,128)} %get-tuple-element.209) | copy-start | bytes 25165828 | tf_op jit(solution)/shard_map/while
  123.9 3.4 copy-start.1
  127.3 7.8 %slice-start = ((s8[8388608]{0:T(1024)(128)(4,1)}), s8[4194304]{0:T(1024)(128)(4,1)S(1)}, s32[]{:S(2)}) async-start(s8[8388608]{0:T(1024)(128)(4,1)} %bitcast.128), calls=%async_computation.12 | async-start | bytes 8388608 | tf_op jit(solution)/shard_map/while
  129.4 5.8 %slice-start.1 = ((s8[8388608]{0:T(1024)(128)(4,1)}), s8[4194304]{0:T(1024)(128)(4,1)S(1)}, s32[]{:S(2)}) async-start(s8[8388608]{0:T(1024)(128)(4,1)} %bitcast.128), calls=%async_computation.13 | async-start | bytes 8388608 | tf_op jit(solution)/shard_map/while
  129.4 5.8 %copy-start.6 = (bf16[2048,2,64]{0,2,1:T(8,128)(2,1)S(1)}, bf16[2048,2,64]{0,2,1:T(8,128)(2,1)}, u32[]{:S(2)}) copy-start(bf16[2048,2,64]{0,2,1:T(8,128)(2,1)} %get-tuple-element.243) | copy-start | bytes 1572868 | tf_op jit(solution)/shard_map/while
  142.2 6.0 %copy-start.2 = (f32[2,512,2048]{2,1,0:T(8,128)S(1)}, f32[2,512,2048]{2,1,0:T(8,128)}, u32[]{:S(2)}) copy-start(f32[2,512,2048]{2,1,0:T(8,128)} %get-tuple-element.209) | copy-start | bytes 25165828 | tf_op jit(solution)/shard_map/while
  151.1 3.4 copy-start.1
  154.6 7.8 %slice-start = ((s8[8388608]{0:T(1024)(128)(4,1)}), s8[4194304]{0:T(1024)(128)(4,1)S(1)}, s32[]{:S(2)}) async-start(s8[8388608]{0:T(1024)(128)(4,1)} %bitcast.128), calls=%async_computation.12 | async-start | bytes 8388608 | tf_op jit(solution)/shard_map/while
  156.6 5.8 %slice-start.1 = ((s8[8388608]{0:T(1024)(128)(4,1)}), s8[4194304]{0:T(1024)(128)(4,1)S(1)}, s32[]{:S(2)}) async-start(s8[8388608]{0:T(1024)(128)(4,1)} %bitcast.128), calls=%async_computation.13 | async-start | bytes 8388608 | tf_op jit(solution)/shard_map/while
  156.6 5.8 %copy-start.6 = (bf16[2048,2,64]{0,2,1:T(8,128)(2,1)S(1)}, bf16[2048,2,64]{0,2,1:T(8,128)(2,1)}, u32[]{:S(2)}) copy-start(bf16[2048,2,64]{0,2,1:T(8,128)(2,1)} %get-tuple-element.243) | copy-start | bytes 1572868 | tf_op jit(solution)/shard_map/while
  169.5 6.0 %copy-start.2 = (f32[2,512,2048]{2,1,0:T(8,128)S(1)}, f32[2,512,2048]{2,1,0:T(8,128)}, u32[]{:S(2)}) copy-start(f32[2,512,2048]{2,1,0:T(8,128)} %get-tuple-element.209) | copy-start | bytes 25165828 | tf_op jit(solution)/shard_map/while
  178.4 3.4 copy-start.1
  181.8 7.8 %slice-start = ((s8[8388608]{0:T(1024)(128)(4,1)}), s8[4194304]{0:T(1024)(128)(4,1)S(1)}, s32[]{:S(2)}) async-start(s8[8388608]{0:T(1024)(128)(4,1)} %bitcast.128), calls=%async_computation.12 | async-start | bytes 8388608 | tf_op jit(solution)/shard_map/while
  183.9 5.8 %slice-start.1 = ((s8[8388608]{0:T(1024)(128)(4,1)}), s8[4194304]{0:T(1024)(128)(4,1)S(1)}, s32[]{:S(2)}) async-start(s8[8388608]{0:T(1024)(128)(4,1)} %bitcast.128), calls=%async_computation.13 | async-start | bytes 8388608 | tf_op jit(solution)/shard_map/while
  183.9 5.8 %copy-start.6 = (bf16[2048,2,64]{0,2,1:T(8,128)(2,1)S(1)}, bf16[2048,2,64]{0,2,1:T(8,128)(2,1)}, u32[]{:S(2)}) copy-start(bf16[2048,2,64]{0,2,1:T(8,128)(2,1)} %get-tuple-element.243) | copy-start | bytes 1572868 | tf_op jit(solution)/shard_map/while
  208.6 4.6 %copy-start.7 = (bf16[4,512,2,64]{1,3,2,0:T(8,128)(2,1)S(1)}, bf16[4,512,2,64]{1,3,2,0:T(8,128)(2,1)}, u32[]{:S(2)}) copy-start(bf16[4,512,2,64]{1,3,2,0:T(8,128)(2,1)} %get-tuple-element.52) | copy-start | bytes 1572868
  214.7 12.5 %all-to-all-start.4 = ((bf16[8,256,128]{1,2,0:T(8,128)(2,1)}), bf16[8,256,128]{1,2,0:T(8,128)(2,1)S(1)}, u32[]{:S(2)}, u32[]{:S(2)}) async-start(bf16[8,256,128]{1,2,0:T(8,128)(2,1)} %copy.61), calls=%async_computation.4 | async-start | bytes 1048576 | tf_op jit(solution)/shard_map/all_to_all | solution.py:77
  227.1 23.4 %all-to-all-start.5 = ((bf16[8,256,128]{1,2,0:T(8,128)(2,1)}), bf16[8,256,128]{1,2,0:T(8,128)(2,1)S(1)}, u32[]{:S(2)}, u32[]{:S(2)}) async-start(bf16[8,256,128]{1,2,0:T(8,128)(2,1)} %copy.62), calls=%async_computation.5 | async-start | bytes 1048576 | tf_op jit(solution)/shard_map/all_to_all | solution.py:78
  250.5 40.1 %copy-start.4 = (bf16[8,256,128]{1,2,0:T(8,128)(2,1)}, bf16[8,256,128]{1,2,0:T(8,128)(2,1)S(1)}, u32[]{:S(2)}) copy-start(bf16[8,256,128]{1,2,0:T(8,128)(2,1)S(1)} %all-to-all-done.5) | copy-start | bytes 1572868
  250.5 40.1 %all-to-all-start.6 = ((bf16[8,256,128]{1,2,0:T(8,128)(2,1)}), bf16[8,256,128]{1,2,0:T(8,128)(2,1)S(1)}, u32[]{:S(2)}, u32[]{:S(2)}) async-start(bf16[8,256,128]{1,2,0:T(8,128)(2,1)} %copy.63), calls=%async_computation.6 | async-start | bytes 1048576 | tf_op jit(solution)/shard_map/all_to_all | solution.py:79
  254.0 122.7 %all-reduce.2.cloned.1.call-start = ((), (), s32[]{:S(2)}) async-start(), calls=%async_computation.11 | async-start | bytes 1048576 | tf_op jit(solution)/shard_map/psum | solution.py:90
  290.6 0.8 copy-start.5
Sparse Core Ops, SparseCore 0:
  9.7 43.6 all-gather.1
  213.3 77.2 reduce-scatter.1
  293.1 83.6 all-reduce.1
where the time goes:
time: 391 us; the launch traced here: 385 us
  waiting for transfers between devices  172 us (44%)
  matrix products  101 us (26%)
  local copies, waits for them, and re-layouts  37.8 us (10%)
  starting transfers between devices  30.4 us (8%)
  blocking collectives  15.2 us (4%)
  other arithmetic  14.4 us (4%)
  between operations  14 us (4%)
    psum x1, waiting for transfers between devices, on_device(): grad_weight = lax.psum(share, 'seq')  82.3 us
    reduce_scatter x1, waiting for transfers between devices, on_device(): lax.psum_scatter(lax.dot_general(token_out, grad_tokens, (((0,), (0,)), (...  36.5 us
    dot_general x4, matrix products, attend_block(): jnp.einsum('hqk,qhd->khd', probs_low, grad_rows, preferred_element_type=j...  22.7 us
    dot_general x4, matrix products, attend_block(): jnp.einsum('qhd,khd->hqk', grad_rows, values_head, preferred_element_type...  20.6 us
    sub x4, matrix products, attend_block(): exp_scores = jnp.exp(scores - row_max)  19.7 us
    all_to_all x1, waiting for transfers between devices, on_device(): lax.all_to_all(head_dk, 'seq', split_axis=0, concat_axis=1, tiled=True)  17.6 us
    all_to_all x1, blocking collectives, on_device(): lax.all_to_all(head_out, 'seq', split_axis=0, concat_axis=1, tiled=True)  15.2 us
    unnamed x19, local copies, waits for them, and re-layouts  13.8 us
  transfers between devices with their start and end apart: 10, of which 8 were waited for; matrix products, arithmetic and copies ran while one was open for 8% of the time, Pallas kernels for 0%

commit v1 on v0

v1 whole, which is shorter than its diff:
```python
import math

import jax
import jax.numpy as jnp
from jax import lax
from jax.experimental import pallas as pl
from jax.experimental.pallas import tpu as pltpu
from jax.sharding import PartitionSpec as P

HEAD_DIM = 64

ROWS = 256
CHUNK = 512
LANES = 128
EXP_SCALE = HEAD_DIM ** (-0.5) * math.log2(math.e)
F32 = jnp.float32
BF16 = jnp.bfloat16


def split_heads(columns):
    row = lax.broadcasted_iota(jnp.int32, columns.shape, 0)
    zeros = jnp.zeros_like(columns)
    return jnp.concatenate(
        [jnp.where(row < HEAD_DIM, columns, zeros), jnp.where(row < HEAD_DIM, zeros, columns)], axis=1
    )


def merge_heads(wide):
    first, second = wide[:, :ROWS], wide[:, ROWS:]
    row = lax.broadcasted_iota(jnp.int32, first.shape, 0)
    return jnp.where(row < HEAD_DIM, first, second)


def dot(a, b):
    return jnp.dot(a, b, preferred_element_type=F32)


def attention_kernel(
    q_ref, k_ref, v_ref, g_ref, out_ref, dq_ref, dk_ref, dv_ref,
    k_t, v_t, score, prob, q_t, out_t, inv_sum, out_all, g_t, q_l, g_l, dq_t, dk_sum, dv_sum,
):
    blocks = q_ref.shape[0]
    length = blocks * ROWS
    chunks = length // CHUNK
    wide = 2 * ROWS
    k_rows = k_ref.reshape(length, LANES)
    v_rows = v_ref.reshape(length, LANES)
    for i in range(blocks):
        k_t[:, i * ROWS : (i + 1) * ROWS] = k_ref[i].astype(F32).T.astype(BF16)
        v_t[:, i * ROWS : (i + 1) * ROWS] = v_ref[i].astype(F32).T.astype(BF16)
    dk_sum[...] = jnp.zeros_like(dk_sum)
    dv_sum[...] = jnp.zeros_like(dv_sum)

    def forward(i, carry):
        q_t[...] = split_heads(q_ref[i].astype(F32).T).astype(BF16)

        def score_chunk(c, top):
            keys = pl.ds(pl.multiple_of(c * CHUNK, CHUNK), CHUNK)
            s = dot(k_rows[keys, :], q_t[...])
            score[keys, :] = s
            return jnp.maximum(top, jnp.max(s.reshape(CHUNK // 8, 8, wide), axis=0))

        top = lax.fori_loop(0, chunks, score_chunk, jnp.full((8, wide), -jnp.inf, F32), unroll=True)
        top = jnp.max(top, axis=0, keepdims=True)
        out_t[...] = jnp.zeros_like(out_t)

        def prob_chunk(c, total):
            keys = pl.ds(pl.multiple_of(c * CHUNK, CHUNK), CHUNK)
            p = jnp.exp2((score[keys, :] - top) * EXP_SCALE)
            low = p.astype(BF16)
            prob[i, keys, :] = low
            out_t[...] += dot(v_t[:, keys], low)
            return total + jnp.sum(p.reshape(CHUNK // 8, 8, wide), axis=0)

        total = lax.fori_loop(0, chunks, prob_chunk, jnp.zeros((8, wide), F32), unroll=True)
        inverse = 1.0 / jnp.sum(total, axis=0, keepdims=True)
        inv_sum[i] = jnp.broadcast_to(inverse, (8, wide))
        merged = merge_heads(out_t[...] * inverse)
        out_all[i] = merged
        out_ref[i] = merged.T.astype(BF16)
        return carry

    lax.fori_loop(0, blocks, forward, 0)

    def backward(i, carry):
        inverse = inv_sum[i, 0:1, :]
        g = g_ref[i].astype(F32).T
        g_split = split_heads(g)
        g_t[...] = g_split.astype(BF16)
        g_l[...] = (g_split * inverse).T.astype(BF16)
        q_l[...] = (split_heads(q_ref[i].astype(F32).T) * (inverse * HEAD_DIM ** (-0.5))).T.astype(BF16)
        product = out_all[i] * g
        row_dot = jnp.concatenate(
            [
                jnp.sum(product[:HEAD_DIM], axis=0, keepdims=True),
                jnp.sum(product[HEAD_DIM:], axis=0, keepdims=True),
            ],
            axis=1,
        )
        dq_t[...] = jnp.zeros_like(dq_t)

        def grad_chunk(c, carry):
            keys = pl.ds(pl.multiple_of(c * CHUNK, CHUNK), CHUNK)
            grad_prob = dot(v_rows[keys, :], g_t[...])
            low = prob[i, keys, :]
            grad_score = (low.astype(F32) * (grad_prob - row_dot)).astype(BF16)
            dv_sum[keys, :] += dot(low, g_l[...])
            dk_sum[keys, :] += dot(grad_score, q_l[...])
            dq_t[...] += dot(k_t[:, keys], grad_score)
            return carry

        lax.fori_loop(0, chunks, grad_chunk, 0, unroll=True)
        dq_ref[i] = merge_heads(dq_t[...] * (inverse * HEAD_DIM ** (-0.5))).T.astype(BF16)
        return carry

    lax.fori_loop(0, blocks, backward, 0)
    dk_ref[...] = dk_sum[...].astype(BF16).reshape(dk_ref.shape)
    dv_ref[...] = dv_sum[...].astype(BF16).reshape(dv_ref.shape)


def attention(q, k, v, g):
    length, columns = q.shape
    blocks = length // ROWS
    shape = (blocks, ROWS, columns)
    vmem = pltpu.VMEM
    results = pl.pallas_call(
        attention_kernel,
        out_shape=[jax.ShapeDtypeStruct(shape, BF16)] * 4,
        in_specs=[pl.BlockSpec(memory_space=vmem)] * 4,
        out_specs=[pl.BlockSpec(memory_space=vmem)] * 4,
        scratch_shapes=[
            vmem((LANES, length), BF16),
            vmem((LANES, length), BF16),
            vmem((length, 2 * ROWS), F32),
            vmem((blocks, length, 2 * ROWS), BF16),
            vmem((LANES, 2 * ROWS), BF16),
            vmem((LANES, 2 * ROWS), F32),
            vmem((blocks, 8, 2 * ROWS), F32),
            vmem((blocks, LANES, ROWS), F32),
            vmem((LANES, 2 * ROWS), BF16),
            vmem((2 * ROWS, LANES), BF16),
            vmem((2 * ROWS, LANES), BF16),
            vmem((LANES, 2 * ROWS), F32),
            vmem((length, LANES), F32),
            vmem((length, LANES), F32),
        ],
        compiler_params=pltpu.CompilerParams(vmem_limit_bytes=48 << 20),
    )(*(x.reshape(shape) for x in (q, k, v, g)))
    return [x.reshape(length, columns) for x in results]


def on_device(queries, keys, values, out_proj, grad_out):
    grad_tokens = grad_out[0]
    grad_attn = lax.dot_general(
        grad_tokens,
        lax.all_gather(out_proj, "dp", axis=0, tiled=True),
        (((1,), (1,)), ((), ())),
        preferred_element_type=jnp.float32,
    ).astype(jnp.bfloat16)
    head_q, head_k, head_v, head_g = (
        lax.all_to_all(queries[0], "seq", split_axis=1, concat_axis=0, tiled=True),
        lax.all_to_all(keys[0], "seq", split_axis=1, concat_axis=0, tiled=True),
        lax.all_to_all(values[0], "seq", split_axis=1, concat_axis=0, tiled=True),
        lax.all_to_all(grad_attn, "seq", split_axis=1, concat_axis=0, tiled=True),
    )
    head_out, head_dq, head_dk, head_dv = attention(head_q, head_k, head_v, head_g)
    token_out, token_dq, token_dk, token_dv = (
        lax.all_to_all(head_out, "seq", split_axis=0, concat_axis=1, tiled=True),
        lax.all_to_all(head_dq, "seq", split_axis=0, concat_axis=1, tiled=True),
        lax.all_to_all(head_dk, "seq", split_axis=0, concat_axis=1, tiled=True),
        lax.all_to_all(head_dv, "seq", split_axis=0, concat_axis=1, tiled=True),
    )
    grad_qkv = jnp.concatenate([token_dq, token_dk, token_dv], axis=1)[None]
    share = lax.psum_scatter(
        lax.dot_general(
            token_out, grad_tokens, (((0,), (0,)), ((), ())), preferred_element_type=jnp.float32
        ),
        "dp",
        scatter_dimension=0,
        tiled=True,
    )
    grad_weight = lax.psum(share, "seq")
    return (grad_qkv, grad_weight)


def solution(mesh):
    return jax.shard_map(
        on_device,
        mesh=mesh,
        in_specs=(
            P("dp", "seq", None),
            P("dp", "seq", None),
            P("dp", "seq", None),
            P("dp", None),
            P("dp", "seq", None),
        ),
        out_specs=(P("dp", "seq", None), P("dp", None)),
        check_vma=False,
    )
```

time: 391 us -> 304 us (0.78)
  matrix products: 101 us -> 7.95 us
  blocking collectives: 15.2 us -> 52.8 us
  Pallas kernels: 0 us -> 35.6 us
  local copies, waits for them, and re-layouts: 37.8 us -> 14.9 us
  waiting for transfers between devices: 172 us -> 151 us
  other arithmetic: 14.4 us -> 1.3 us
  starting transfers between devices: 30.4 us -> 20.7 us
    dot_general x20 -> x0, matrix products: 73.3 us -> none  [the longest x4 22.7 us: attend_block(): jnp.einsum('hqk,qhd->khd', probs_low, grad_rows, preferred_element_type=j...]
    all_to_all x0 -> x3, blocking collectives: none -> 41.3 us  [the longest x1 17.1 us: on_device(): lax.all_to_all(head_dk, 'seq', split_axis=0, concat_axis=1, tiled=True)]
    pallas_call x0 -> x1, Pallas kernels: none -> 35.6 us  [attention(): pl.pallas_call(attention_kernel, out_shape=[jax.ShapeDtypeStruct(shape, B...]
    all_to_all x3 -> x0, waiting for transfers between devices: 25.5 us -> none  [the longest x1 17.6 us: on_device(): lax.all_to_all(head_dk, 'seq', split_axis=0, concat_axis=1, tiled=True)]
    sub x4 -> x0, matrix products: 19.7 us -> none  [attend_block(): exp_scores = jnp.exp(scores - row_max)]
    convert_element_type x6 -> x0, other arithmetic: 13.1 us -> none  [the longest x4 11.8 us: attend_block(): grad_score = (scaling * probs * (grad_prob - row_dot)).astype(jnp.bfloat16)]
    all_to_all x3 -> x0, starting transfers between devices: 11.1 us -> none  [the longest x1 4.14 us: on_device(): lax.all_to_all(grad_attn, 'seq', split_axis=1, concat_axis=0, tiled=True)]
    reshape x4 -> x0, local copies, waits for them, and re-layouts: 7.76 us -> none  [the longest x1 2.18 us: on_device(): query_blocks = head_q.reshape(blocks, block_rows, local_heads, HEAD_DIM)]
  transfers between devices with their start and end apart: 10 -> 7, of which waited for: 8 -> 6; matrix products, arithmetic and copies ran while one was open for 8% -> 5% of each run, Pallas kernels for 0% -> 0%
where the time goes in v1:
time: 304 us; the launch traced here: 298 us
  waiting for transfers between devices  151 us (50%)
  blocking collectives  52.8 us (17%)
  Pallas kernels  35.6 us (12%)
  starting transfers between devices  20.7 us (7%)
  local copies, waits for them, and re-layouts  14.9 us (5%)
  between operations  13.8 us (5%)
  matrix products  7.95 us (3%)
    psum x1, waiting for transfers between devices, on_device(): grad_weight = lax.psum(share, 'seq')  80.5 us
    reduce_scatter x1, waiting for transfers between devices, on_device(): lax.psum_scatter(lax.dot_general(token_out, grad_tokens, (((0,), (0,)), (...  41.9 us
    pallas_call x1, Pallas kernels, attention(): pl.pallas_call(attention_kernel, out_shape=[jax.ShapeDtypeStruct(shape, B...  35.6 us
    all_to_all x1, blocking collectives, on_device(): lax.all_to_all(head_dk, 'seq', split_axis=0, concat_axis=1, tiled=True)  17.1 us
    all_to_all x1, waiting for transfers between devices, on_device(): lax.all_to_all(keys[0], 'seq', split_axis=1, concat_axis=0, tiled=True)  14.7 us
    all_to_all x1, blocking collectives, on_device(): lax.all_to_all(grad_attn, 'seq', split_axis=1, concat_axis=0, tiled=True)  12.8 us
    all_to_all x1, blocking collectives, on_device(): lax.all_to_all(head_out, 'seq', split_axis=0, concat_axis=1, tiled=True)  11.4 us
    all_to_all x1, blocking collectives, on_device(): lax.all_to_all(head_dq, 'seq', split_axis=0, concat_axis=1, tiled=True)  11.4 us
  transfers between devices with their start and end apart: 7, of which 6 were waited for; matrix products, arithmetic and copies ran while one was open for 5% of the time, Pallas kernels for 0%

profile of v1, /device:TPU:1, one launch (start us, length us, event | category | flops | bytes accessed | tf_op | source)
XLA Modules:
  0.0 298.5 jit_solution(12926245243233538292)
XLA Ops:
  7.2 0.0 copy-start
  7.2 0.0 copy-start.3
  7.2 0.0 all-gather.2.cloned.1.call-start
  7.2 0.7 all-gather.2.cloned.1.call-update
  7.9 0.0 copy-start.4
  7.9 1.3 copy.7
  9.2 1.0 copy.8
  10.2 8.5 %all-to-all-start = ((bf16[256,8,128]{2,0,1:T(8,128)(2,1)}), bf16[256,8,128]{2,0,1:T(8,128)(2,1)S(1)}, u32[]{:S(2)}, u32[]{:S(2)}) async-start(bf16[256,8,128]{2,0,1:T(8,128)(2,1)} %copy.8), calls=%async_computation | async-start | bytes 1048576 | tf_op jit(solution)/shard_map/all_to_all | solution.py:161
  18.7 0.0 copy-done.3
  18.7 0.2 copy.9
  18.9 1.0 copy.10
  19.9 10.5 %all-to-all-done = bf16[256,8,128]{2,0,1:T(8,128)(2,1)S(1)} async-done(((bf16[256,8,128]{2,0,1:T(8,128)(2,1)}), bf16[256,8,128]{2,0,1:T(8,128)(2,1)S(1)}, u32[]{:S(2)}, u32[]{:S(2)}) %all-to-all-start) | async-done | bytes 524320 | tf_op jit(solution)/shard_map/all_to_all | solution.py:161
  30.5 3.5 %all-to-all-start.1 = ((bf16[256,8,128]{2,0,1:T(8,128)(2,1)}), bf16[256,8,128]{2,0,1:T(8,128)(2,1)S(1)}, u32[]{:S(2)}, u32[]{:S(2)}) async-start(bf16[256,8,128]{2,0,1:T(8,128)(2,1)} %copy.10), calls=%async_computation.1 | async-start | bytes 1048576 | tf_op jit(solution)/shard_map/all_to_all | solution.py:162
  34.0 0.0 copy-done.4
  34.0 0.2 copy.11
  34.2 1.0 copy.12
  35.2 14.7 %all-to-all-done.1 = bf16[256,8,128]{2,0,1:T(8,128)(2,1)S(1)} async-done(((bf16[256,8,128]{2,0,1:T(8,128)(2,1)}), bf16[256,8,128]{2,0,1:T(8,128)(2,1)S(1)}, u32[]{:S(2)}, u32[]{:S(2)}) %all-to-all-start.1) | async-done | bytes 524320 | tf_op jit(solution)/shard_map/all_to_all | solution.py:162
  49.9 3.5 %all-to-all-start.2 = ((bf16[256,8,128]{2,0,1:T(8,128)(2,1)}), bf16[256,8,128]{2,0,1:T(8,128)(2,1)S(1)}, u32[]{:S(2)}, u32[]{:S(2)}) async-start(bf16[256,8,128]{2,0,1:T(8,128)(2,1)} %copy.12), calls=%async_computation.2 | async-start | bytes 1048576 | tf_op jit(solution)/shard_map/all_to_all | solution.py:163
  53.4 0.0 reduce-scatter.2.cloned.1.call-start
  53.4 0.2 all-gather.2.cloned.1.call-done
  53.6 0.0 copy-done
  53.6 3.5 %convolution_convert_fusion = bf16[256,1024]{1,0:T(8,128)(2,1)S(1)} fusion(bf16[1024,2048]{1,0:T(8,128)(2,1)} %all-gather.2.cloned.1.call-done, bf16[1,256,2048]{2,1,0:T(8,128)(2,1)S(1)} %copy-done), kind=kOutput, calls=%fused_computation.1 | convolution fusion | flops 1074003968 | bytes 5767168 | tf_op jit(solution)/shard_map/dot_general | solution.py:154
  57.1 1.0 copy.13
  58.1 1.3 copy.14
  59.4 2.9 all-to-all-done.2
  62.4 12.8 %all_to_all.128 = bf16[256,8,128]{2,0,1:T(8,128)(2,1)S(1)} all-to-all(bf16[256,8,128]{2,0,1:T(8,128)(2,1)S(1)} %copy.14), channel_id=1, replica_groups=mesh['seq'=8,'dp'=16] {'seq'}, dimensions={1} | all-to-all | bytes 1048576 | tf_op jit(solution)/shard_map/all_to_all | solution.py:164
  75.1 35.6 %shard_map.68 = (bf16[8,256,128]{2,1,0:T(8,128)(2,1)S(1)}, bf16[8,256,128]{2,1,0:T(8,128)(2,1)S(1)}, bf16[8,256,128]{2,1,0:T(8,128)(2,1)S(1)}, bf16[8,256,128]{2,1,0:T(8,128)(2,1)}) custom-call(bf16[8,256,128]{2,1,0:T(8,128)(2,1)S(1)} %bitcast.25, bf16[8,256,128]{2,1,0:T(8,128)(2,1)S(1)} %bitcast.26, bf16[8,256,128]{2,1,0:T(8,128)(2,1)S(1)} %bitcast.27, ...), custom_call_target="tpu_custom_call" | custom-call | tf_op jit(solution)/shard_map/pallas_call | solution.py:126
  110.8 0.0 copy-start.1
  110.8 0.8 copy-done.1
  111.6 11.4 %all_to_all.129 = bf16[8,256,128]{2,1,0:T(8,128)(2,1)S(1)} all-to-all(bf16[8,256,128]{2,1,0:T(8,128)(2,1)S(1)} %get-tuple-element.9), channel_id=1, replica_groups=mesh['seq'=8,'dp'=16] {'seq'}, dimensions={0} | all-to-all | bytes 1048576 | tf_op jit(solution)/shard_map/all_to_all | solution.py:168
  123.0 0.2 copy.18
  123.2 4.5 %fusion = f32[1024,2048]{1,0:T(8,128)} fusion(bf16[256,1024]{0,1:T(8,128)(2,1)S(1)} %bitcast.29, bf16[1,256,2048]{2,1,0:T(8,128)(2,1)S(1)} %copy-done), kind=kOutput, calls=%fused_computation.2 | convolution fusion | flops 1073741824 | bytes 9961472 | tf_op jit(solution)/shard_map/dot_general | solution.py:175
  127.7 0.0 reduce-scatter.2.cloned.1.call-update
  127.7 1.0 copy-done.2
  128.8 11.4 %all_to_all.130 = bf16[8,256,128]{2,1,0:T(8,128)(2,1)S(1)} all-to-all(bf16[8,256,128]{2,1,0:T(8,128)(2,1)S(1)} %copy-done.2), channel_id=1, replica_groups=mesh['seq'=8,'dp'=16] {'seq'}, dimensions={0} | all-to-all | bytes 1048576 | tf_op jit(solution)/shard_map/all_to_all | solution.py:169
  140.2 17.1 %all_to_all.131 = bf16[8,256,128]{2,1,0:T(8,128)(2,1)S(1)} all-to-all(bf16[8,256,128]{2,1,0:T(8,128)(2,1)S(1)} %get-tuple-element.7), channel_id=1, replica_groups=mesh['seq'=8,'dp'=16] {'seq'}, dimensions={0} | all-to-all | bytes 1048576 | tf_op jit(solution)/shard_map/all_to_all | solution.py:170
  157.3 5.0 %all-to-all-start.6 = ((bf16[8,256,128]{2,1,0:T(8,128)(2,1)}), bf16[8,256,128]{2,1,0:T(8,128)(2,1)S(1)}, u32[]{:S(2)}, u32[]{:S(2)}) async-start(bf16[8,256,128]{2,1,0:T(8,128)(2,1)} %get-tuple-element.8), calls=%async_computation.6 | async-start | bytes 1048576 | tf_op jit(solution)/shard_map/all_to_all | solution.py:171
  162.4 0.0 all-reduce.2.cloned.1.call-start
  162.4 41.9 %reduce-scatter.2.cloned.1.call-done = f32[64,2048]{1,0:T(8,128)} async-done(((f32[1024,2048]{1,0:T(8,128)}), f32[64,2048]{1,0:T(8,128)}) %reduce-scatter.2.cloned.1.call-update) | async-done | bytes 524304 | tf_op jit(solution)/shard_map/reduce_scatter | solution.py:174
  204.3 0.0 all-reduce.2.cloned.1.call-update
  204.3 0.2 copy.15
  204.5 1.0 copy.16
  205.5 0.0 all-to-all-done.6
  205.5 1.0 copy.17
  206.6 1.3 maximum_bitcast_fusion
  207.9 1.7 copy.19
  209.6 80.5 %all-reduce.2.cloned.1.call-done = f32[64,2048]{1,0:T(8,128)} async-done(((f32[64,2048]{1,0:T(8,128)}), f32[64,2048]{1,0:T(8,128)}) %all-reduce.2.cloned.1.call-update) | async-done | bytes 524304 | tf_op jit(solution)/shard_map/psum | solution.py:182
  290.1 1.9 copy.21
  (1 shorter events, 0.0 us)
Async XLA Ops:
  7.2 46.5 %copy-start = (bf16[1,256,2048]{2,1,0:T(8,128)(2,1)S(1)}, bf16[1,256,2048]{2,1,0:T(8,128)(2,1)}, u32[]{:S(2)}) copy-start(bf16[1,256,2048]{2,1,0:T(8,128)(2,1)} %param.9) | copy-start | bytes 3145732
  7.2 11.6 %copy-start.3 = (bf16[1,256,1024]{2,1,0:T(8,128)(2,1)S(1)}, bf16[1,256,1024]{2,1,0:T(8,128)(2,1)}, u32[]{:S(2)}) copy-start(bf16[1,256,1024]{2,1,0:T(8,128)(2,1)} %param.6) | copy-start | bytes 1572868
  7.2 46.5 %all-gather.2.cloned.1.call-start = ((), (), s32[]{:S(2)}) async-start(), calls=%async_computation.9 | async-start | bytes 4456448 | tf_op jit(solution)/shard_map/all_gather | solution.py:156
  7.9 26.0 %copy-start.4 = (bf16[1,256,1024]{2,1,0:T(8,128)(2,1)S(1)}, bf16[1,256,1024]{2,1,0:T(8,128)(2,1)}, u32[]{:S(2)}) copy-start(bf16[1,256,1024]{2,1,0:T(8,128)(2,1)} %param.7) | copy-start | bytes 1572868
  10.2 20.2 %all-to-all-start = ((bf16[256,8,128]{2,0,1:T(8,128)(2,1)}), bf16[256,8,128]{2,0,1:T(8,128)(2,1)S(1)}, u32[]{:S(2)}, u32[]{:S(2)}) async-start(bf16[256,8,128]{2,0,1:T(8,128)(2,1)} %copy.8), calls=%async_computation | async-start | bytes 1048576 | tf_op jit(solution)/shard_map/all_to_all | solution.py:161
  30.5 19.4 %all-to-all-start.1 = ((bf16[256,8,128]{2,0,1:T(8,128)(2,1)}), bf16[256,8,128]{2,0,1:T(8,128)(2,1)S(1)}, u32[]{:S(2)}, u32[]{:S(2)}) async-start(bf16[256,8,128]{2,0,1:T(8,128)(2,1)} %copy.10), calls=%async_computation.1 | async-start | bytes 1048576 | tf_op jit(solution)/shard_map/all_to_all | solution.py:162
  49.9 12.5 %all-to-all-start.2 = ((bf16[256,8,128]{2,0,1:T(8,128)(2,1)}), bf16[256,8,128]{2,0,1:T(8,128)(2,1)S(1)}, u32[]{:S(2)}, u32[]{:S(2)}) async-start(bf16[256,8,128]{2,0,1:T(8,128)(2,1)} %copy.12), calls=%async_computation.2 | async-start | bytes 1048576 | tf_op jit(solution)/shard_map/all_to_all | solution.py:163
  53.4 150.9 %reduce-scatter.2.cloned.1.call-start = ((), (), s32[]{:S(2)}) async-start(), calls=%async_computation.10 | async-start | bytes 8912896 | tf_op jit(solution)/shard_map/reduce_scatter | solution.py:174
  110.8 0.8 copy-start.1
  127.7 1.0 copy-start.2
  157.3 48.2 %all-to-all-start.6 = ((bf16[8,256,128]{2,1,0:T(8,128)(2,1)}), bf16[8,256,128]{2,1,0:T(8,128)(2,1)S(1)}, u32[]{:S(2)}, u32[]{:S(2)}) async-start(bf16[8,256,128]{2,1,0:T(8,128)(2,1)} %get-tuple-element.8), calls=%async_computation.6 | async-start | bytes 1048576 | tf_op jit(solution)/shard_map/all_to_all | solution.py:171
  162.4 127.7 %all-reduce.2.cloned.1.call-start = ((), (), s32[]{:S(2)}) async-start(), calls=%async_computation.11 | async-start | bytes 1048576 | tf_op jit(solution)/shard_map/psum | solution.py:182
Sparse Core Ops, SparseCore 0:
  9.7 43.8 all-gather.1
  127.9 76.3 reduce-scatter.1
  206.8 83.2 all-reduce.1

commit v2 on v1

v2 whole, which is shorter than its diff:
```python
import functools
import math

import jax
import jax.numpy as jnp
from jax import lax
from jax.experimental import pallas as pl
from jax.experimental.pallas import tpu as pltpu
from jax.sharding import PartitionSpec as P

HEAD_DIM = 64
LANES = 2 * HEAD_DIM
CHUNK = 512
SCALING = HEAD_DIM ** (-0.5)
EXP_SCALE = SCALING * math.log2(math.e)
F32 = jnp.float32
BF16 = jnp.bfloat16


def dot(a, b):
    return jnp.dot(a, b, preferred_element_type=F32)


def dot_nt(a, b):
    return lax.dot_general(a, b, (((1,), (1,)), ((), ())), preferred_element_type=F32)


def split_heads(columns):
    row = lax.broadcasted_iota(jnp.int32, columns.shape, 0)
    zeros = jnp.zeros_like(columns)
    return jnp.concatenate(
        [jnp.where(row < HEAD_DIM, columns, zeros), jnp.where(row < HEAD_DIM, zeros, columns)], axis=1
    )


def merge_heads(wide):
    rows = wide.shape[1] // 2
    first, second = wide[:, :rows], wide[:, rows:]
    row = lax.broadcasted_iota(jnp.int32, first.shape, 0)
    return jnp.where(row < HEAD_DIM, first, second)


def kernel(
    n, rows, width,
    q_ref, k_ref, v_ref, w_ref, go_ref, dqkv_ref, gw_ref,
    q_in, k_in, v_in, g_in, w_all, go, k_t, v_t,
    score, prob, q_t, out_t, inv_sum, out_all, g_t, q_l, g_l, dq_t, dk_sum, dv_sum,
    g_out, o_out, o_in, o_rows, own_part, sib_out, sib_in, rs_out, rs_in,
    total, total_low, gs_in, done, dq_out, dk_out, dv_out,
    qkv_send, qkv_recv, w_send, w_recv, ws_send, ws_recv, g_send, g_recv, o_send, o_recv,
    sib_send, sib_recv, rs_send, rs_recv, gs_send, gs_recv, gw_send, gw_recv,
    d_send, d_recv, local_sem,
):
    s = lax.axis_index("seq")
    d = lax.axis_index("dp")
    chip, core = d // 2, lax.rem(d, 2)
    length = n * rows
    chunks = length // CHUNK
    wide = 2 * rows
    half = HEAD_DIM
    columns = width // n

    def ahead(base, i):
        return lax.rem(base + i, n)

    def behind(base, i):
        return lax.rem(base + n - i, n)

    def block(index, size):
        return pl.ds(pl.multiple_of(index * size, size), size)

    def remote(src, dst, send, recv, where):
        return pltpu.make_async_remote_copy(
            src_ref=src, dst_ref=dst, send_sem=send, recv_sem=recv,
            device_id=where, device_id_type=pl.DeviceIdType.MESH,
        )

    my_half = block(core, half)
    sibling = {"dp": 2 * chip + 1 - core}

    def qkv_copy(t, i):
        src, dst = ((k_ref, k_in), (v_ref, v_in), (q_ref, q_in))[t]
        peer = ahead(s, i)
        return remote(
            src.at[0, :, block(peer, LANES)], dst.at[i], qkv_send.at[t, i], qkv_recv.at[t, i], {"seq": peer}
        )

    def w_copy(j):
        return remote(
            w_ref, w_all.at[j, my_half, :], w_send.at[j], w_recv.at[j], {"dp": 2 * ahead(chip, j) + core}
        )

    def ws_first():
        return remote(w_ref, w_all.at[0, my_half, :], ws_send.at[0], ws_recv.at[0], sibling)

    def ws_copy(j):
        part = w_all.at[j, my_half, :]
        return remote(part, part, ws_send.at[j], ws_recv.at[j], sibling)

    def g_copy(i):
        return remote(g_out.at[i], g_in.at[i], g_send.at[i], g_recv.at[i], {"seq": ahead(s, i)})

    def o_copy(i):
        return remote(o_out.at[i], o_in.at[i], o_send.at[i], o_recv.at[i], {"seq": behind(s, i)})

    def sib_copy():
        return remote(sib_out, sib_in, sib_send.at[0], sib_recv.at[0], sibling)

    def rs_copy(j):
        return remote(
            rs_out.at[j], rs_in.at[j], rs_send.at[j], rs_recv.at[j], {"dp": 2 * ahead(chip, j) + core}
        )

    def gs_copy(i):
        peer = ahead(s, i)
        return remote(total_low.at[peer], gs_in.at[i], gs_send.at[i], gs_recv.at[i], {"seq": peer})

    def gw_copy(i):
        return remote(
            done, gw_ref.at[:, block(s, columns)], gw_send.at[i], gw_recv.at[i], {"seq": ahead(s, i)}
        )

    def d_copy(t, i):
        src = (dq_out, dk_out, dv_out)[t]
        dst = dqkv_ref.at[0, :, block(t * n + s, LANES)]
        return remote(src.at[i], dst, d_send.at[t, i], d_recv.at[t, i], {"seq": behind(s, i)})

    def each(first, step):
        def body(i, carry):
            step(i)
            return carry

        lax.fori_loop(first, n, body, 0)

    local = [
        pltpu.make_async_copy(k_ref.at[0, :, block(s, LANES)], k_in.at[0], local_sem.at[0]),
        pltpu.make_async_copy(v_ref.at[0, :, block(s, LANES)], v_in.at[0], local_sem.at[1]),
        pltpu.make_async_copy(q_ref.at[0, :, block(s, LANES)], q_in.at[0], local_sem.at[2]),
        pltpu.make_async_copy(w_ref, w_all.at[0, my_half, :], local_sem.at[3]),
        pltpu.make_async_copy(go_ref.at[0], go, local_sem.at[4]),
    ]
    for copy in local:
        copy.start()

    barrier = pltpu.get_barrier_semaphore()

    def greet(i):
        pl.semaphore_signal(
            barrier, inc=1, device_id={"seq": ahead(s, i)}, device_id_type=pl.DeviceIdType.MESH
        )
        pl.semaphore_signal(
            barrier, inc=1, device_id={"dp": 2 * ahead(chip, i) + core}, device_id_type=pl.DeviceIdType.MESH
        )

    each(1, greet)
    pl.semaphore_signal(barrier, inc=1, device_id=sibling, device_id_type=pl.DeviceIdType.MESH)
    pl.semaphore_wait(barrier, 2 * (n - 1) + 1)

    def send_first(i):
        qkv_copy(0, i).start()
        w_copy(i).start()

    ws_first().start()
    each(1, send_first)
    each(1, lambda i: qkv_copy(1, i).start())
    each(1, lambda i: qkv_copy(2, i).start())
    for copy in local:
        copy.wait()

    dk_sum[...] = jnp.zeros_like(dk_sum)
    dv_sum[...] = jnp.zeros_like(dv_sum)

    def turn(src, dst, i):
        dst[:, block(i, rows)] = src[i].astype(F32).T.astype(BF16)

    turn(k_in, k_t, 0)
    turn(v_in, v_t, 0)

    def arrive(i):
        qkv_copy(0, i).wait_recv()
        turn(k_in, k_t, i)
        qkv_copy(1, i).wait_recv()
        turn(v_in, v_t, i)

    each(1, arrive)

    k_rows = k_in.reshape(length, LANES)
    v_rows = v_in.reshape(length, LANES)

    def grad_attn(j):
        peer = behind(chip, j)
        i = behind(peer, s)
        g = dot_nt(go[...], w_all[j]).astype(BF16)

        @pl.when(i == 0)
        def _():
            g_in[0] = g

        @pl.when(i > 0)
        def _():
            g_out[i] = g
            g_copy(i).start()

    def forward(i, carry):
        @pl.when(i > 0)
        def _():
            qkv_copy(2, i).wait_recv()

        q_t[...] = split_heads(q_in[i].astype(F32).T).astype(BF16)

        def score_chunk(c, top):
            keys = block(c, CHUNK)
            x = dot(k_rows[keys, :], q_t[...])
            score[keys, :] = x
            return jnp.maximum(top, jnp.max(x.reshape(CHUNK // 8, 8, wide), axis=0))

        top = lax.fori_loop(0, chunks, score_chunk, jnp.full((8, wide), -jnp.inf, F32), unroll=True)
        top = jnp.max(top, axis=0, keepdims=True)
        out_t[...] = jnp.zeros_like(out_t)

        def prob_chunk(c, norm):
            keys = block(c, CHUNK)
            p = jnp.exp2((score[keys, :] - top) * EXP_SCALE)
            low = p.astype(BF16)
            prob[i, keys, :] = low
            out_t[...] += dot(v_t[:, keys], low)
            return norm + jnp.sum(p.reshape(CHUNK // 8, 8, wide), axis=0)

        norm = lax.fori_loop(0, chunks, prob_chunk, jnp.zeros((8, wide), F32), unroll=True)
        inverse = 1.0 / jnp.sum(norm, axis=0, keepdims=True)
        inv_sum[i] = jnp.broadcast_to(inverse, (8, wide))
        merged = merge_heads(out_t[...] * inverse)
        out_all[i] = merged

        @pl.when(i == 0)
        def _():
            o_in[0] = merged.astype(BF16)

        @pl.when(i > 0)
        def _():
            o_out[i] = merged.astype(BF16)
            o_copy(i).start()
            w_copy(i).wait_recv()
            ws_copy(i).start()
            ws_copy(i - 1).wait_recv()
            grad_attn(i - 1)

        return carry

    lax.fori_loop(0, n, forward, 0)
    ws_copy(n - 1).wait_recv()
    grad_attn(n - 1)

    def weight_part():
        each(1, lambda i: o_copy(i).wait_recv())
        for i in range(n):
            o_rows[i * half : (i + 1) * half, :] = o_in[i, my_half, :]
            o_rows[(n + i) * half : (n + i + 1) * half, :] = o_in[i, block(1 - core, half), :]
        for c in range(n):
            cut = slice(c * columns, (c + 1) * columns)
            part = dot(o_rows[...], go[:, cut])
            own_part[:, :, cut] = part[: n * half].reshape(n, half, columns).astype(BF16)
            sib_out[:, :, cut] = part[n * half :].reshape(n, half, columns).astype(BF16)
        sib_copy().start()

    def pair_sum(j):
        i = behind(ahead(chip, j), s)
        return own_part[i].astype(F32) + sib_in[i].astype(F32)

    def share():
        sib_copy().wait_recv()

        def send(j):
            rs_out[j] = pair_sum(j).astype(BF16)
            rs_copy(j).start()

        each(1, send)

    def backward(i, carry):
        @pl.when(i > 0)
        def _():
            g_copy(i).wait_recv()

        inverse = inv_sum[i, 0:1, :]
        g = g_in[i].astype(F32).T
        g_split = split_heads(g)
        g_t[...] = g_split.astype(BF16)
        g_l[...] = (g_split * inverse).T.astype(BF16)
        q_l[...] = (split_heads(q_in[i].astype(F32).T) * (inverse * SCALING)).T.astype(BF16)
        product = out_all[i] * g
        row_dot = jnp.concatenate(
            [
                jnp.sum(product[:half], axis=0, keepdims=True),
                jnp.sum(product[half:], axis=0, keepdims=True),
            ],
            axis=1,
        )
        dq_t[...] = jnp.zeros_like(dq_t)

        def grad_chunk(c, carry):
            keys = block(c, CHUNK)
            grad_prob = dot(v_rows[keys, :], g_t[...])
            low = prob[i, keys, :]
            grad_score = (low.astype(F32) * (grad_prob - row_dot)).astype(BF16)
            dv_sum[keys, :] += dot(low, g_l[...])
            dk_sum[keys, :] += dot(grad_score, q_l[...])
            dq_t[...] += dot(k_t[:, keys], grad_score)
            return carry

        lax.fori_loop(0, chunks, grad_chunk, 0, unroll=True)
        grad_q = merge_heads(dq_t[...] * (inverse * SCALING)).T.astype(BF16)

        @pl.when(i == 0)
        def _():
            dqkv_ref[0, :, block(s, LANES)] = grad_q
            weight_part()

        @pl.when(i > 0)
        def _():
            dq_out[i] = grad_q
            d_copy(0, i).start()

        @pl.when(i == 1)
        def _():
            share()

        return carry

    lax.fori_loop(0, n, backward, 0)

    dqkv_ref[0, :, block(n + s, LANES)] = dk_sum[0:rows, :].astype(BF16)
    dqkv_ref[0, :, block(2 * n + s, LANES)] = dv_sum[0:rows, :].astype(BF16)

    def finish(i):
        dk_out[i] = dk_sum[block(i, rows), :].astype(BF16)
        d_copy(1, i).start()
        dv_out[i] = dv_sum[block(i, rows), :].astype(BF16)
        d_copy(2, i).start()

    each(1, finish)

    each(1, lambda j: rs_copy(j).wait_recv())
    mine = behind(chip, s)
    for c in range(n):
        cut = slice(c * columns, (c + 1) * columns)
        x = own_part[mine, :, cut].astype(F32) + sib_in[mine, :, cut].astype(F32)
        for j in range(1, n):
            x += rs_in[j, :, cut].astype(F32)
        total[c] = x
        total_low[c] = x.astype(BF16)
    each(1, lambda i: gs_copy(i).start())
    each(1, lambda i: gs_copy(i).wait_recv())
    x = total[s]
    for i in range(1, n):
        x += gs_in[i].astype(F32)
    done[...] = x
    each(1, lambda i: gw_copy(i).start())
    gw_ref[:, block(s, columns)] = x

    def arrivals(i):
        gw_copy(i).wait_recv()
        for t in range(3):
            d_copy(t, i).wait_recv()

    each(1, arrivals)

    def sent(i):
        for t in range(3):
            qkv_copy(t, i).wait_send()
            d_copy(t, i).wait_send()
        w_copy(i).wait_send()
        ws_copy(i).wait_send()
        g_copy(i).wait_send()
        o_copy(i).wait_send()
        rs_copy(i).wait_send()
        gs_copy(i).wait_send()
        gw_copy(i).wait_send()

    ws_first().wait_send()
    sib_copy().wait_send()
    each(1, sent)


def on_device(n, queries, keys, values, out_proj, grad_out):
    rows, features = queries.shape[1:]
    share_rows, width = out_proj.shape
    length = n * rows
    wide = 2 * rows
    columns = width // n
    vmem = pltpu.VMEM
    dma = pltpu.SemaphoreType.DMA
    flat = vmem((n, rows, LANES), BF16)
    turned = vmem((n, LANES, rows), BF16)
    shares = vmem((n, HEAD_DIM, width), BF16)
    return pl.pallas_call(
        functools.partial(kernel, n, rows, width),
        out_shape=(
            jax.ShapeDtypeStruct((1, rows, 3 * features), BF16),
            jax.ShapeDtypeStruct((share_rows, width), F32),
        ),
        in_specs=[pl.BlockSpec(memory_space=pl.ANY)] * 5,
        out_specs=[pl.BlockSpec(memory_space=vmem)] * 2,
        scratch_shapes=[
            flat, flat, flat, flat,
            vmem((n, LANES, width), BF16),
            vmem((rows, width), BF16),
            vmem((LANES, length), BF16),
            vmem((LANES, length), BF16),
            vmem((length, wide), F32),
            vmem((n, length, wide), BF16),
            vmem((LANES, wide), BF16),
            vmem((LANES, wide), F32),
            vmem((n, 8, wide), F32),
            vmem((n, LANES, rows), F32),
            vmem((LANES, wide), BF16),
            vmem((wide, LANES), BF16),
            vmem((wide, LANES), BF16),
            vmem((LANES, wide), F32),
            vmem((length, LANES), F32),
            vmem((length, LANES), F32),
            flat, turned, turned,
            vmem((2 * n * HEAD_DIM, rows), BF16),
            shares, shares, shares, shares, shares,
            vmem((n, HEAD_DIM, columns), F32),
            vmem((n, HEAD_DIM, columns), BF16),
            vmem((n, HEAD_DIM, columns), BF16),
            vmem((HEAD_DIM, columns), F32),
            flat, flat, flat,
            dma((3, n)), dma((3, n)),
            dma((n,)), dma((n,)), dma((n,)), dma((n,)),
            dma((n,)), dma((n,)), dma((n,)), dma((n,)),
            dma((1,)), dma((1,)), dma((n,)), dma((n,)),
            dma((n,)), dma((n,)), dma((n,)), dma((n,)),
            dma((3, n)), dma((3, n)), dma((5,)),
        ],
        compiler_params=pltpu.CompilerParams(
            collective_id=0, has_side_effects=True, vmem_limit_bytes=60 << 20
        ),
    )(queries, keys, values, out_proj, grad_out)


def solution(mesh):
    return jax.shard_map(
        functools.partial(on_device, mesh.shape["seq"]),
        mesh=mesh,
        in_specs=(
            P("dp", "seq", None),
            P("dp", "seq", None),
            P("dp", "seq", None),
            P("dp", None),
            P("dp", "seq", None),
        ),
        out_specs=(P("dp", "seq", None), P("dp", None)),
        check_vma=False,
    )
```

time: 304 us -> 137 us (0.45); the launches traced: 298 us -> 136 us
  waiting for transfers between devices: 151 us -> 0 us
  Pallas kernels: 35.6 us -> 131 us
  blocking collectives: 52.8 us -> 0 us
  starting transfers between devices: 20.7 us -> 0 us
  between operations: 13.8 us -> 0.65 us
  local copies, waits for them, and re-layouts: 14.9 us -> 3.51 us
  matrix products: 7.95 us -> 0 us
    pallas_call x1, Pallas kernels: 35.6 us -> 131 us  [on_device(): pl.pallas_call(functools.partial(kernel, n, rows, width), out_shape=(jax....]
    psum x1 -> x0, waiting for transfers between devices: 80.5 us -> none  [on_device(): grad_weight = lax.psum(share, 'seq')]
    all_to_all x4 -> x0, blocking collectives: 52.8 us -> none  [the longest x1 17.1 us: on_device(): lax.all_to_all(head_dk, 'seq', split_axis=0, concat_axis=1, tiled=True)]
    reduce_scatter x1 -> x0, waiting for transfers between devices: 41.9 us -> none  [on_device(): lax.psum_scatter(lax.dot_general(token_out, grad_tokens, (((0,), (0,)), (...]
    all_to_all x4 -> x0, waiting for transfers between devices: 28.2 us -> none  [the longest x1 14.7 us: on_device(): lax.all_to_all(keys[0], 'seq', split_axis=1, concat_axis=0, tiled=True)]
    all_to_all x4 -> x0, starting transfers between devices: 20.5 us -> none  [the longest x1 8.49 us: on_device(): lax.all_to_all(queries[0], 'seq', split_axis=1, concat_axis=0, tiled=True)]
    dot_general x2 -> x0, matrix products: 7.95 us -> none  [the longest x1 4.49 us: on_device(): lax.dot_general(token_out, grad_tokens, (((0,), (0,)), ((), ())), preferr...]
    all_to_all x8 -> x0, local copies, waits for them, and re-layouts: 6.75 us -> none  [the longest x1 1.31 us: on_device(): lax.all_to_all(grad_attn, 'seq', split_axis=1, concat_axis=0, tiled=True)]
  transfers between devices with their start and end apart: 7 -> 0, of which waited for: 6 -> 0; matrix products, arithmetic and copies ran while one was open for 5% -> 0% of each run, Pallas kernels for 0% -> 0%
where the time goes in v2:
time: 137 us; the launch traced here: 136 us
  Pallas kernels  131 us (96%)
  local copies, waits for them, and re-layouts  3.51 us (3%)
    pallas_call x1, Pallas kernels, on_device(): pl.pallas_call(functools.partial(kernel, n, rows, width), out_shape=(jax....  131 us
    unnamed x4, local copies, waits for them, and re-layouts  3.51 us

profile of v2, /device:TPU:1, one launch (start us, length us, event | category | flops | bytes accessed | tf_op | source)
XLA Modules:
  0.0 135.6 jit_solution(16501065322762271454)
XLA Ops:
  0.6 131.5 %shard_map.68 = (bf16[1,256,3072]{2,1,0:T(8,128)(2,1)}, f32[64,2048]{1,0:T(8,128)}) custom-call(bf16[1,256,1024]{2,1,0:T(8,128)(2,1)} %q_ref.1, bf16[1,256,1024]{2,1,0:T(8,128)(2,1)} %k_ref.1, bf16[1,256,1024]{2,1,0:T(8,128)(2,1)} %v_ref.1, bf16[64,2048]{1,0:T(8,128)(2,1)} %w_ref.1, bf16[1,256,2048]{2,1,0:T(8,128)(2,1)} %go_ref.1), custom_call_target="tpu_custom_call" | custom-call | tf_op jit(solution)/shard_map/pallas_call | solution.py:395
  132.1 0.0 copy-start
  132.1 2.7 %copy.9 = bf16[1,256,3072]{2,1,0:T(8,128)(2,1)} copy(bf16[1,256,3072]{2,1,0:T(8,128)(2,1)} %get-tuple-element.4) | data formatting | bytes 3145728
  134.8 0.0 copy-done
  134.8 0.8 copy.10
Async XLA Ops:
  132.1 2.7 %copy-start = (f32[64,2048]{1,0:T(8,128)S(1)}, f32[64,2048]{1,0:T(8,128)}, u32[]{:S(2)}) copy-start(f32[64,2048]{1,0:T(8,128)} %get-tuple-element.5) | copy-start | bytes 1572868

commit v3 on v2

v3 whole, which is shorter than its diff:
```python
import functools
import math

import jax
import jax.numpy as jnp
from jax import lax
from jax.experimental import pallas as pl
from jax.experimental.pallas import tpu as pltpu
from jax.sharding import PartitionSpec as P

HEAD_DIM = 64
LANES = 2 * HEAD_DIM
X = 4
CHUNK = 512
SCALING = HEAD_DIM ** (-0.5)
EXP_SCALE = SCALING * math.log2(math.e)
F32 = jnp.float32
BF16 = jnp.bfloat16


def dot(a, b):
    return jnp.dot(a, b, preferred_element_type=F32)


def dot_nt(a, b):
    return lax.dot_general(a, b, (((1,), (1,)), ((), ())), preferred_element_type=F32)


def split_heads(columns):
    row = lax.broadcasted_iota(jnp.int32, columns.shape, 0)
    zeros = jnp.zeros_like(columns)
    return jnp.concatenate(
        [jnp.where(row < HEAD_DIM, columns, zeros), jnp.where(row < HEAD_DIM, zeros, columns)], axis=1
    )


def merge_heads(wide):
    rows = wide.shape[1] // 2
    first, second = wide[:, :rows], wide[:, rows:]
    row = lax.broadcasted_iota(jnp.int32, first.shape, 0)
    return jnp.where(row < HEAD_DIM, first, second)


def kernel(
    n, rows, width,
    q_ref, k_ref, v_ref, w_ref, go_ref, dqkv_ref, gw_ref,
    q_in, k_in, v_in, g_in, w_all, go, k_t, v_t,
    score, prob, q_t, out_t, inv_sum, out_all, row_dot, g_t, g_l, q_l, ds_buf, dq_t,
    g_out, o_out, o_in, o_rows, own_part, sib_out, sib_in, rs_out, rs_in, home, y_out, y_in,
    total, total_low, gs_in, done, dq_out, dk_out, dv_out,
    qkv_send, qkv_recv, w_send, w_recv, ws_send, ws_recv, g_send, g_recv, o_send, o_recv,
    sib_send, sib_recv, rs_send, rs_recv, y_send, y_recv, gs_send, gs_recv, gw_send, gw_recv,
    d_send, d_recv, local_sem,
):
    s = lax.axis_index("seq")
    d = lax.axis_index("dp")
    chip, core = d // 2, lax.rem(d, 2)
    y, x = chip // X, lax.rem(chip, X)
    length = n * rows
    chunks = length // CHUNK
    wide = 2 * rows
    half = HEAD_DIM
    columns = width // n
    batch = n // 2

    def ahead(base, i):
        return lax.rem(base + i, n)

    def behind(base, i):
        return lax.rem(base + n - i, n)

    def block(index, size):
        return pl.ds(pl.multiple_of(index * size, size), size)

    def remote(src, dst, send, recv, where):
        return pltpu.make_async_remote_copy(
            src_ref=src, dst_ref=dst, send_sem=send, recv_sem=recv,
            device_id=where, device_id_type=pl.DeviceIdType.MESH,
        )

    my_half = block(core, half)
    sibling = {"dp": 2 * chip + 1 - core}

    def chip_at(dy, dx):
        return lax.rem(y + dy, 2) * X + lax.rem(x + dx, X)

    def device_at(dy, dx):
        return {"dp": 2 * chip_at(dy, dx) + core}

    def qkv_copy(t, i):
        src, dst = ((k_ref, k_in), (v_ref, v_in), (q_ref, q_in))[t]
        peer = ahead(s, i)
        return remote(
            src.at[0, :, block(peer, LANES)], dst.at[i], qkv_send.at[t, i], qkv_recv.at[t, i], {"seq": peer}
        )

    def w_copy(slot):
        src = {7: 4, 5: 4, 2: 3, 6: 5}.get(slot)
        dy, dx = {3: (0, 1), 1: (0, 3), 4: (1, 0), 7: (0, 1), 5: (0, 3), 2: (0, 1), 6: (0, 3)}[slot]
        return remote(
            w_ref if src is None else w_all.at[src, my_half, :],
            w_all.at[slot, my_half, :], w_send.at[slot], w_recv.at[slot], device_at(dy, dx),
        )

    def ws_copy(slot):
        part = w_all.at[slot, my_half, :]
        return remote(w_ref if slot == 0 else part, part, ws_send.at[slot], ws_recv.at[slot], sibling)

    def g_copy(i):
        return remote(g_out.at[i], g_in.at[i], g_send.at[i], g_recv.at[i], {"seq": ahead(s, i)})

    def o_copy(i):
        return remote(o_out.at[i], o_in.at[i], o_send.at[i], o_recv.at[i], {"seq": behind(s, i)})

    def sib_copy(b):
        part = pl.ds(b * batch, batch)
        return remote(sib_out.at[part], sib_in.at[part], sib_send.at[b], sib_recv.at[b], sibling)

    def where_to(i):
        h = ahead(s, i)
        return lax.rem(h // X + y, 2), lax.rem(lax.rem(h, X) + X - x, X)

    def rs_copy(i):
        dy, dx = where_to(i)
        slot = dy * X + lax.rem(X - dx, X)
        return remote(rs_out.at[i], rs_in.at[slot], rs_send.at[i], rs_recv.at[slot], device_at(0, dx))

    def rs_arrival(slot):
        return remote(rs_out.at[0], rs_in.at[slot], rs_send.at[0], rs_recv.at[slot], device_at(0, 1))

    def y_copy():
        return remote(y_out, y_in, y_send.at[0], y_recv.at[0], device_at(1, 0))

    def gs_copy(i):
        peer = ahead(s, i)
        return remote(total_low.at[peer], gs_in.at[i], gs_send.at[i], gs_recv.at[i], {"seq": peer})

    def gw_copy(i):
        return remote(
            done, gw_ref.at[:, block(s, columns)], gw_send.at[i], gw_recv.at[i], {"seq": ahead(s, i)}
        )

    def d_copy(t, i):
        src = (dq_out, dk_out, dv_out)[t]
        dst = dqkv_ref.at[0, :, block(t * n + s, LANES)]
        return remote(src.at[i], dst, d_send.at[t, i], d_recv.at[t, i], {"seq": behind(s, i)})

    def each(first, step, last=n):
        def body(i, carry):
            step(i)
            return carry

        lax.fori_loop(first, last, body, 0)

    local = [
        pltpu.make_async_copy(k_ref.at[0, :, block(s, LANES)], k_in.at[0], local_sem.at[0]),
        pltpu.make_async_copy(v_ref.at[0, :, block(s, LANES)], v_in.at[0], local_sem.at[1]),
        pltpu.make_async_copy(q_ref.at[0, :, block(s, LANES)], q_in.at[0], local_sem.at[2]),
        pltpu.make_async_copy(w_ref, w_all.at[0, my_half, :], local_sem.at[3]),
        pltpu.make_async_copy(go_ref.at[0], go, local_sem.at[4]),
    ]
    for copy in local:
        copy.start()

    barrier = pltpu.get_barrier_semaphore()

    def greet(where):
        pl.semaphore_signal(barrier, inc=1, device_id=where, device_id_type=pl.DeviceIdType.MESH)

    each(1, lambda i: greet({"seq": ahead(s, i)}))
    for dx in range(1, X):
        greet(device_at(0, dx))
    greet(device_at(1, 0))
    greet(sibling)
    pl.semaphore_wait(barrier, n - 1 + X - 1 + 2)

    for slot in (4, 3, 1):
        w_copy(slot).start()
    for t in range(3):
        each(1, lambda i: qkv_copy(t, i).start())
    ws_copy(0).start()
    for copy in local:
        copy.wait()

    def turn(src, dst, i):
        dst[:, block(i, rows)] = src[i].astype(F32).T.astype(BF16)

    def arrive(t, src, dst, i):
        qkv_copy(t, i).wait_recv()
        turn(src, dst, i)

    def hand_on(slot, *nexts):
        w_copy(slot).wait_recv()
        for following in nexts:
            w_copy(following).start()
        ws_copy(slot).start()

    turn(k_in, k_t, 0)
    turn(v_in, v_t, 0)
    hand_on(4, 7, 5)
    each(1, functools.partial(arrive, 0, k_in, k_t))
    hand_on(3, 2)
    hand_on(1)
    each(1, functools.partial(arrive, 1, v_in, v_t))
    hand_on(5, 6)
    hand_on(7)

    k_rows = k_in.reshape(length, LANES)
    v_rows = v_in.reshape(length, LANES)

    def grad_attn(slot):
        ws_copy(slot).wait_recv()
        i = behind(chip_at(slot // X, slot % X), s)
        g = dot_nt(go[...], w_all[slot]).astype(BF16)

        @pl.when(i == 0)
        def _():
            g_in[0] = g

        @pl.when(i > 0)
        def _():
            g_out[i] = g
            g_copy(i).start()

    def weight_part(b):
        first = b * batch
        each(max(first, 1), lambda i: o_copy(i).wait_recv(), first + batch)
        for i in range(batch):
            o_rows[i * half : (i + 1) * half, :] = o_in[first + i, my_half, :]
            o_rows[(batch + i) * half : (batch + i + 1) * half, :] = o_in[first + i, block(1 - core, half), :]
        for c in range(n):
            cut = slice(c * columns, (c + 1) * columns)
            part = dot(o_rows[...], go[:, cut]).astype(BF16)
            own_part[first : first + batch, :, cut] = part[: batch * half].reshape(batch, half, columns)
            sib_out[first : first + batch, :, cut] = part[batch * half :].reshape(batch, half, columns)
        sib_copy(b).start()

    def share(b):
        sib_copy(b).wait_recv()

        def send(i):
            dy, dx = where_to(i)
            pair = own_part[i].astype(F32) + sib_in[i].astype(F32)

            @pl.when(dx == 0)
            def _():
                home[dy] = pair

            @pl.when(dx > 0)
            def _():
                rs_out[i] = pair.astype(BF16)
                rs_copy(i).start()

        each(b * batch, send, (b + 1) * batch)

    def row_sum():
        for slot in range(1, 2 * X):
            if slot != X:
                rs_arrival(slot).wait_recv()
        for c in range(n):
            cut = slice(c * columns, (c + 1) * columns)
            for dy in (1, 0):
                value = home[dy, :, cut]
                for dx in range(1, X):
                    value += rs_in[dy * X + dx, :, cut].astype(F32)
                if dy:
                    y_out[:, cut] = value.astype(BF16)
                else:
                    total[c] = value
        y_copy().start()

    def chip_sum():
        y_copy().wait_recv()
        for c in range(n):
            value = total[c] + y_in[:, c * columns : (c + 1) * columns].astype(F32)
            total[c] = value
            total_low[c] = value.astype(BF16)
        each(1, lambda i: gs_copy(i).start())

    def weight_out():
        each(1, lambda i: gs_copy(i).wait_recv())
        value = total[s]
        for i in range(1, n):
            value += gs_in[i].astype(F32)
        done[...] = value
        each(1, lambda i: gw_copy(i).start())
        gw_ref[:, block(s, columns)] = value

    def forward(i, carry):
        @pl.when(i > 0)
        def _():
            qkv_copy(2, i).wait_recv()

        queries = split_heads(q_in[i].astype(F32).T)
        q_t[...] = queries.astype(BF16)

        def score_chunk(c, top):
            keys = block(c, CHUNK)
            value = dot(k_rows[keys, :], q_t[...])
            score[keys, :] = value
            return jnp.maximum(top, jnp.max(value.reshape(CHUNK // 8, 8, wide), axis=0))

        top = lax.fori_loop(0, chunks, score_chunk, jnp.full((8, wide), -jnp.inf, F32), unroll=True)
        top = jnp.max(top, axis=0, keepdims=True)
        out_t[...] = jnp.zeros_like(out_t)

        def prob_chunk(c, norm):
            keys = block(c, CHUNK)
            p = jnp.exp2((score[keys, :] - top) * EXP_SCALE)
            low = p.astype(BF16)
            prob[keys, block(i, wide)] = low
            out_t[...] += dot(v_t[:, keys], low)
            return norm + jnp.sum(p.reshape(CHUNK // 8, 8, wide), axis=0)

        norm = lax.fori_loop(0, chunks, prob_chunk, jnp.zeros((8, wide), F32), unroll=True)
        inverse = 1.0 / jnp.sum(norm, axis=0, keepdims=True)
        inv_sum[i] = jnp.broadcast_to(inverse, (8, wide))
        q_l[block(i, wide), :] = (split_heads(q_in[i].astype(F32).T) * (inverse * SCALING)).T.astype(BF16)
        merged = merge_heads(out_t[...] * inverse)
        out_all[i] = merged

        @pl.when(i == 0)
        def _():
            o_in[0] = merged.astype(BF16)

        @pl.when(i > 0)
        def _():
            o_out[i] = merged.astype(BF16)
            o_copy(i).start()

        @pl.when(i == 0)
        def _():
            grad_attn(0)
            grad_attn(4)

        @pl.when(i == 1)
        def _():
            hand_on(2)
            hand_on(6)
            grad_attn(3)
            grad_attn(1)

        @pl.when(i == 2)
        def _():
            grad_attn(5)
            grad_attn(7)

        @pl.when(i == 3)
        def _():
            grad_attn(2)
            grad_attn(6)

        @pl.when(i == batch)
        def _():
            weight_part(0)

        @pl.when(i == batch + 1)
        def _():
            share(0)

        return carry

    lax.fori_loop(0, n, forward, 0)
    weight_part(1)

    def prepare(i, carry):
        @pl.when(i > 0)
        def _():
            g_copy(i).wait_recv()

        g = g_in[i].astype(F32).T
        g_split = split_heads(g)
        g_t[:, block(i, wide)] = g_split.astype(BF16)
        g_l[block(i, wide), :] = (g_split * inv_sum[i, 0:1, :]).T.astype(BF16)
        product = out_all[i] * g
        both = jnp.concatenate(
            [
                jnp.sum(product[:half], axis=0, keepdims=True),
                jnp.sum(product[half:], axis=0, keepdims=True),
            ],
            axis=1,
        )
        row_dot[i] = jnp.broadcast_to(both, (8, wide))
        return carry

    lax.fori_loop(0, n, prepare, 0)
    share(1)
    dq_t[...] = jnp.zeros_like(dq_t)

    def backward(j, carry):
        keys = block(j, rows)

        def grad_chunk(i, carry):
            cut = block(i, wide)
            grad_prob = dot(v_rows[keys, :], g_t[:, cut])
            grad_score = (prob[keys, cut].astype(F32) * (grad_prob - row_dot[i, 0:1, :])).astype(BF16)
            ds_buf[:, cut] = grad_score
            dq_t[:, cut] += dot(k_t[:, keys], grad_score)
            return carry

        lax.fori_loop(0, n, grad_chunk, 0, unroll=True)
        grad_v = dot(prob[keys, :], g_l[...]).astype(BF16)
        grad_k = dot(ds_buf[...], q_l[...]).astype(BF16)

        @pl.when(j == 0)
        def _():
            dqkv_ref[0, :, block(n + s, LANES)] = grad_k
            dqkv_ref[0, :, block(2 * n + s, LANES)] = grad_v

        @pl.when(j > 0)
        def _():
            dk_out[j] = grad_k
            d_copy(1, j).start()
            dv_out[j] = grad_v
            d_copy(2, j).start()

        @pl.when(j == n - 4)
        def _():
            row_sum()

        @pl.when(j == n - 2)
        def _():
            chip_sum()

        return carry

    lax.fori_loop(0, n, backward, 0)

    def grad_q(i):
        return merge_heads(dq_t[:, block(i, wide)] * (inv_sum[i, 0:1, :] * SCALING)).T.astype(BF16)

    def finish(i):
        dq_out[i] = grad_q(i)
        d_copy(0, i).start()

    each(1, finish)
    dqkv_ref[0, :, block(s, LANES)] = grad_q(0)
    weight_out()

    def arrivals(i):
        for t in range(3):
            d_copy(t, i).wait_recv()
        gw_copy(i).wait_recv()

    each(1, arrivals)

    def sent(i):
        for t in range(3):
            qkv_copy(t, i).wait_send()
            d_copy(t, i).wait_send()
        g_copy(i).wait_send()
        o_copy(i).wait_send()
        gs_copy(i).wait_send()
        gw_copy(i).wait_send()

    each(1, sent)
    for slot in range(n):
        if slot:
            w_copy(slot).wait_send()
        ws_copy(slot).wait_send()
    sib_copy(0).wait_send()
    sib_copy(1).wait_send()
    y_copy().wait_send()

    def rs_sent(i):
        @pl.when(where_to(i)[1] > 0)
        def _():
            rs_copy(i).wait_send()

    each(0, rs_sent)


def on_device(n, queries, keys, values, out_proj, grad_out):
    rows, features = queries.shape[1:]
    share_rows, width = out_proj.shape
    length = n * rows
    wide = 2 * rows
    columns = width // n
    vmem = pltpu.VMEM
    dma = pltpu.SemaphoreType.DMA
    flat = vmem((n, rows, LANES), BF16)
    turned = vmem((n, LANES, rows), BF16)
    shares = vmem((n, HEAD_DIM, width), BF16)
    return pl.pallas_call(
        functools.partial(kernel, n, rows, width),
        out_shape=(
            jax.ShapeDtypeStruct((1, rows, 3 * features), BF16),
            jax.ShapeDtypeStruct((share_rows, width), F32),
        ),
        in_specs=[pl.BlockSpec(memory_space=pl.ANY)] * 5,
        out_specs=[pl.BlockSpec(memory_space=vmem)] * 2,
        scratch_shapes=[
            flat, flat, flat, flat,
            vmem((n, LANES, width), BF16),
            vmem((rows, width), BF16),
            vmem((LANES, length), BF16),
            vmem((LANES, length), BF16),
            vmem((length, wide), F32),
            vmem((length, n * wide), BF16),
            vmem((LANES, wide), BF16),
            vmem((LANES, wide), F32),
            vmem((n, 8, wide), F32),
            vmem((n, LANES, rows), F32),
            vmem((n, 8, wide), F32),
            vmem((LANES, n * wide), BF16),
            vmem((n * wide, LANES), BF16),
            vmem((n * wide, LANES), BF16),
            vmem((rows, n * wide), BF16),
            vmem((LANES, n * wide), F32),
            flat, turned, turned,
            vmem((n * HEAD_DIM, rows), BF16),
            shares, shares, shares, shares, shares,
            vmem((2, HEAD_DIM, width), F32),
            vmem((HEAD_DIM, width), BF16),
            vmem((HEAD_DIM, width), BF16),
            vmem((n, HEAD_DIM, columns), F32),
            vmem((n, HEAD_DIM, columns), BF16),
            vmem((n, HEAD_DIM, columns), BF16),
            vmem((HEAD_DIM, columns), F32),
            flat, flat, flat,
            dma((3, n)), dma((3, n)),
            dma((n,)), dma((n,)), dma((n,)), dma((n,)),
            dma((n,)), dma((n,)), dma((n,)), dma((n,)),
            dma((2,)), dma((2,)), dma((n,)), dma((n,)), dma((1,)), dma((1,)),
            dma((n,)), dma((n,)), dma((n,)), dma((n,)),
            dma((3, n)), dma((3, n)), dma((5,)),
        ],
        compiler_params=pltpu.CompilerParams(
            collective_id=0, has_side_effects=True, vmem_limit_bytes=60 << 20
        ),
    )(queries, keys, values, out_proj, grad_out)


def solution(mesh):
    return jax.shard_map(
        functools.partial(on_device, mesh.shape["seq"]),
        mesh=mesh,
        in_specs=(
            P("dp", "seq", None),
            P("dp", "seq", None),
            P("dp", "seq", None),
            P("dp", None),
            P("dp", "seq", None),
        ),
        out_specs=(P("dp", "seq", None), P("dp", None)),
        check_vma=False,
    )
```

time: 137 us -> 120 us (0.88)
  Pallas kernels: 131 us -> 116 us
    pallas_call x1, Pallas kernels: 131 us -> 116 us  [on_device(): pl.pallas_call(functools.partial(kernel, n, rows, width), out_shape=(jax....]
where the time goes in v3:
time: 120 us
  Pallas kernels  116 us (97%)
  local copies, waits for them, and re-layouts  3.51 us (3%)
    pallas_call x1, Pallas kernels, on_device(): pl.pallas_call(functools.partial(kernel, n, rows, width), out_shape=(jax....  116 us
    unnamed x4, local copies, waits for them, and re-layouts  3.51 us

profile of v3, /device:TPU:1, one launch (start us, length us, event | category | flops | bytes accessed | tf_op | source)
XLA Modules:
  0.0 119.8 jit_solution(14788760511014808978)
XLA Ops:
  0.6 115.6 %shard_map.68 = (bf16[1,256,3072]{2,1,0:T(8,128)(2,1)}, f32[64,2048]{1,0:T(8,128)}) custom-call(bf16[1,256,1024]{2,1,0:T(8,128)(2,1)} %q_ref.1, bf16[1,256,1024]{2,1,0:T(8,128)(2,1)} %k_ref.1, bf16[1,256,1024]{2,1,0:T(8,128)(2,1)} %v_ref.1, bf16[64,2048]{1,0:T(8,128)(2,1)} %w_ref.1, bf16[1,256,2048]{2,1,0:T(8,128)(2,1)} %go_ref.1), custom_call_target="tpu_custom_call" | custom-call | tf_op jit(solution)/shard_map/pallas_call | solution.py:484
  116.3 0.0 copy-start
  116.3 2.7 %copy.9 = bf16[1,256,3072]{2,1,0:T(8,128)(2,1)} copy(bf16[1,256,3072]{2,1,0:T(8,128)(2,1)} %get-tuple-element.4) | data formatting | bytes 3145728
  119.0 0.0 copy-done
  119.0 0.8 copy.10
Async XLA Ops:
  116.3 2.7 %copy-start = (f32[64,2048]{1,0:T(8,128)S(1)}, f32[64,2048]{1,0:T(8,128)}, u32[]{:S(2)}) copy-start(f32[64,2048]{1,0:T(8,128)} %get-tuple-element.5) | copy-start | bytes 1572868

commit v4 on v3

--- a/solution.py
+++ b/solution.py
@@ -11,6 +11,9 @@
 HEAD_DIM = 64
 LANES = 2 * HEAD_DIM
 X = 4
+Z = 4
+SPAN = 2
+EARLY = 4
 CHUNK = 512
 SCALING = HEAD_DIM ** (-0.5)
 EXP_SCALE = SCALING * math.log2(math.e)
@@ -44,24 +47,28 @@
 def kernel(
     n, rows, width,
     q_ref, k_ref, v_ref, w_ref, go_ref, dqkv_ref, gw_ref,
-    q_in, k_in, v_in, g_in, w_all, go, k_t, v_t,
+    q_in, k_in, v_in, g_in, w_all, go, go_t, k_t, v_t,
     score, prob, q_t, out_t, inv_sum, out_all, row_dot, g_t, g_l, q_l, ds_buf, dq_t,
-    g_out, o_out, o_in, o_rows, own_part, sib_out, sib_in, rs_out, rs_in, home, y_out, y_in,
-    total, total_low, gs_in, done, dq_out, dk_out, dv_out,
+    g_out, o_out, o_in, o_rows, own_part, sib_out, sib_in, rs_out, rs_in, home,
+    total, zs_out, zs_in, ys_out, ys_in, done, dq_out, dk_out, dv_out,
     qkv_send, qkv_recv, w_send, w_recv, ws_send, ws_recv, g_send, g_recv, o_send, o_recv,
-    sib_send, sib_recv, rs_send, rs_recv, y_send, y_recv, gs_send, gs_recv, gw_send, gw_recv,
+    sib_send, sib_recv, rs_send, rs_recv, zs_send, zs_recv, ys_send, ys_recv, gw_send, gw_recv,
     d_send, d_recv, local_sem,
 ):
     s = lax.axis_index("seq")
     d = lax.axis_index("dp")
     chip, core = d // 2, lax.rem(d, 2)
     y, x = chip // X, lax.rem(chip, X)
+    z, y_hi = s // 2, lax.rem(s, 2)
+    quarter = width // Z
     length = n * rows
     chunks = length // CHUNK
     wide = 2 * rows
     half = HEAD_DIM
     columns = width // n
     batch = n // 2
+    span = SPAN * rows
+    steps = n // SPAN
 
     def ahead(base, i):
         return lax.rem(base + i, n)
@@ -128,16 +135,24 @@
     def rs_arrival(slot):
         return remote(rs_out.at[0], rs_in.at[slot], rs_send.at[0], rs_recv.at[slot], device_at(0, 1))
 
-    def y_copy():
-        return remote(y_out, y_in, y_send.at[0], y_recv.at[0], device_at(1, 0))
-
-    def gs_copy(i):
-        peer = ahead(s, i)
-        return remote(total_low.at[peer], gs_in.at[i], gs_send.at[i], gs_recv.at[i], {"seq": peer})
-
-    def gw_copy(i):
+    def zs_copy(k):
+        to = lax.rem(z + k, Z)
         return remote(
-            done, gw_ref.at[:, block(s, columns)], gw_send.at[i], gw_recv.at[i], {"seq": ahead(s, i)}
+            zs_out.at[to], zs_in.at[k], zs_send.at[k], zs_recv.at[k], {"seq": 2 * to + y_hi}
+        )
+
+    def ys_copy(k):
+        dy, dh = ((1, 0), (1, 1), (0, 1))[k]
+        where = {
+            "seq": 2 * z + lax.rem(y_hi + dh, 2),
+            "dp": 2 * chip_at(dy, 0) + core,
+        }
+        return remote(ys_out.at[dy], ys_in.at[2 * y_hi + y], ys_send.at[k], ys_recv.at[k], where)
+
+    def gw_copy(k):
+        to = lax.rem(z + k, Z)
+        return remote(
+            done, gw_ref.at[:, block(z, quarter)], gw_send.at[k], gw_recv.at[k], {"seq": 2 * to + y_hi}
         )
 
     def d_copy(t, i):
@@ -171,23 +186,23 @@
     for dx in range(1, X):
         greet(device_at(0, dx))
     greet(device_at(1, 0))
+    greet({"seq": 2 * z + 1 - y_hi, **device_at(1, 0)})
     greet(sibling)
-    pl.semaphore_wait(barrier, n - 1 + X - 1 + 2)
+    pl.semaphore_wait(barrier, n - 1 + X - 1 + 3)
 
     for slot in (4, 3, 1):
         w_copy(slot).start()
-    for t in range(3):
+    for t in (0, 2, 1):
         each(1, lambda i: qkv_copy(t, i).start())
     ws_copy(0).start()
     for copy in local:
         copy.wait()
+    for c in range(n):
+        cut = slice(c * columns, (c + 1) * columns)
+        go_t[cut, :] = go[:, cut].astype(F32).T.astype(BF16)
 
     def turn(src, dst, i):
         dst[:, block(i, rows)] = src[i].astype(F32).T.astype(BF16)
-
-    def arrive(t, src, dst, i):
-        qkv_copy(t, i).wait_recv()
-        turn(src, dst, i)
 
     def hand_on(slot, *nexts):
         w_copy(slot).wait_recv()
@@ -195,32 +210,28 @@
             w_copy(following).start()
         ws_copy(slot).start()
 
-    turn(k_in, k_t, 0)
-    turn(v_in, v_t, 0)
     hand_on(4, 7, 5)
-    each(1, functools.partial(arrive, 0, k_in, k_t))
-    hand_on(3, 2)
-    hand_on(1)
-    each(1, functools.partial(arrive, 1, v_in, v_t))
-    hand_on(5, 6)
-    hand_on(7)
+    each(1, lambda i: qkv_copy(0, i).wait_recv())
 
     k_rows = k_in.reshape(length, LANES)
     v_rows = v_in.reshape(length, LANES)
 
-    def grad_attn(slot):
-        ws_copy(slot).wait_recv()
-        i = behind(chip_at(slot // X, slot % X), s)
-        g = dot_nt(go[...], w_all[slot]).astype(BF16)
-
-        @pl.when(i == 0)
-        def _():
-            g_in[0] = g
-
-        @pl.when(i > 0)
-        def _():
-            g_out[i] = g
-            g_copy(i).start()
+    def grad_attn(*slots):
+        for slot in slots:
+            ws_copy(slot).wait_recv()
+        both = dot(jnp.concatenate([w_all[slot] for slot in slots], axis=0), go_t[...]).astype(BF16)
+        for at, slot in enumerate(slots):
+            i = behind(chip_at(slot // X, slot % X), s)
+            g = both[at * LANES : (at + 1) * LANES]
+
+            @pl.when(i == 0)
+            def _():
+                g_in[0] = g
+
+            @pl.when(i > 0)
+            def _():
+                g_out[i] = g
+                g_copy(i).start()
 
     def weight_part(b):
         first = b * batch
@@ -257,42 +268,56 @@
         for slot in range(1, 2 * X):
             if slot != X:
                 rs_arrival(slot).wait_recv()
-        for c in range(n):
-            cut = slice(c * columns, (c + 1) * columns)
-            for dy in (1, 0):
+        for c in range(Z):
+            cut = slice(c * quarter, (c + 1) * quarter)
+            for dy in range(2):
                 value = home[dy, :, cut]
                 for dx in range(1, X):
                     value += rs_in[dy * X + dx, :, cut].astype(F32)
-                if dy:
-                    y_out[:, cut] = value.astype(BF16)
-                else:
-                    total[c] = value
-        y_copy().start()
-
-    def chip_sum():
-        y_copy().wait_recv()
-        for c in range(n):
-            value = total[c] + y_in[:, c * columns : (c + 1) * columns].astype(F32)
-            total[c] = value
-            total_low[c] = value.astype(BF16)
-        each(1, lambda i: gs_copy(i).start())
+                total[c, dy] = value
+                zs_out[c, dy] = value.astype(BF16)
+        for k in range(1, Z):
+            zs_copy(k).start()
+
+    def patch_sum():
+        for k in range(1, Z):
+            zs_copy(k).wait_recv()
+        for dy in range(2):
+            value = total[z, dy]
+            for k in range(1, Z):
+                value += zs_in[k, dy].astype(F32)
+            ys_out[dy] = value.astype(BF16)
+        for k in range(3):
+            ys_copy(k).start()
+        ys_in[2 * y_hi + y] = ys_out[0]
 
     def weight_out():
-        each(1, lambda i: gs_copy(i).wait_recv())
-        value = total[s]
-        for i in range(1, n):
-            value += gs_in[i].astype(F32)
+        for k in range(3):
+            ys_copy(k).wait_recv()
+        value = ys_in[0].astype(F32)
+        for at in range(1, 4):
+            value += ys_in[at].astype(F32)
         done[...] = value
-        each(1, lambda i: gw_copy(i).start())
-        gw_ref[:, block(s, columns)] = value
-
-    def forward(i, carry):
+        for k in range(1, Z):
+            gw_copy(k).start()
+        gw_ref[:, block(z, quarter)] = value
+
+    def column(value):
+        return jnp.broadcast_to(value, (8, wide)).T[:, 0:1]
+
+    def scaled_rows(natural, scale):
+        lane = lax.broadcasted_iota(jnp.int32, natural.shape, 1)
+        first = jnp.where(lane < half, natural * scale[:rows], 0.0)
+        second = jnp.where(lane < half, 0.0, natural * scale[rows:])
+        return jnp.concatenate([first, second], axis=0).astype(BF16)
+
+    def probs(i, with_out):
         @pl.when(i > 0)
         def _():
             qkv_copy(2, i).wait_recv()
 
-        queries = split_heads(q_in[i].astype(F32).T)
-        q_t[...] = queries.astype(BF16)
+        q = q_in[i].astype(F32)
+        q_t[...] = split_heads(q.T).astype(BF16)
 
         def score_chunk(c, top):
             keys = block(c, CHUNK)
@@ -302,21 +327,27 @@
 
         top = lax.fori_loop(0, chunks, score_chunk, jnp.full((8, wide), -jnp.inf, F32), unroll=True)
         top = jnp.max(top, axis=0, keepdims=True)
-        out_t[...] = jnp.zeros_like(out_t)
+        if with_out:
+            out_t[...] = jnp.zeros_like(out_t)
 
         def prob_chunk(c, norm):
             keys = block(c, CHUNK)
             p = jnp.exp2((score[keys, :] - top) * EXP_SCALE)
             low = p.astype(BF16)
             prob[keys, block(i, wide)] = low
-            out_t[...] += dot(v_t[:, keys], low)
+            if with_out:
+                out_t[...] += dot(v_t[:, keys], low)
             return norm + jnp.sum(p.reshape(CHUNK // 8, 8, wide), axis=0)
 
         norm = lax.fori_loop(0, chunks, prob_chunk, jnp.zeros((8, wide), F32), unroll=True)
         inverse = 1.0 / jnp.sum(norm, axis=0, keepdims=True)
         inv_sum[i] = jnp.broadcast_to(inverse, (8, wide))
-        q_l[block(i, wide), :] = (split_heads(q_in[i].astype(F32).T) * (inverse * SCALING)).T.astype(BF16)
-        merged = merge_heads(out_t[...] * inverse)
+        q_l[block(i, wide), :] = scaled_rows(q, column(inverse * SCALING))
+        if with_out:
+            send_out(i, out_t[...] * inverse)
+
+    def send_out(i, wide_out):
+        merged = merge_heads(wide_out)
         out_all[i] = merged
 
         @pl.when(i == 0)
@@ -328,50 +359,67 @@
             o_out[i] = merged.astype(BF16)
             o_copy(i).start()
 
+    def early(i, carry):
+        probs(i, False)
+
         @pl.when(i == 0)
         def _():
-            grad_attn(0)
-            grad_attn(4)
+            hand_on(3, 2)
+            hand_on(1)
+            grad_attn(0, 4)
 
         @pl.when(i == 1)
         def _():
-            hand_on(2)
-            hand_on(6)
-            grad_attn(3)
-            grad_attn(1)
+            hand_on(5, 6)
+            grad_attn(3, 1)
 
         @pl.when(i == 2)
         def _():
-            grad_attn(5)
-            grad_attn(7)
-
-        @pl.when(i == 3)
-        def _():
-            grad_attn(2)
-            grad_attn(6)
-
-        @pl.when(i == batch)
+            hand_on(7)
+
+        return carry
+
+    def late(i, carry):
+        probs(i, True)
+
+        @pl.when(i == EARLY)
+        def _():
+            grad_attn(2, 6)
+
+        @pl.when(i == batch + 1)
         def _():
             weight_part(0)
 
-        @pl.when(i == batch + 1)
+        @pl.when(i == batch + 2)
         def _():
             share(0)
 
         return carry
 
-    lax.fori_loop(0, n, forward, 0)
-    weight_part(1)
+    lax.fori_loop(0, EARLY, early, 0)
+    turn(k_in, k_t, 0)
+    each(1, lambda i: turn(k_in, k_t, i))
+    grad_attn(5, 7)
+    turn(v_in, v_t, 0)
+
+    def arrive(i):
+        qkv_copy(1, i).wait_recv()
+        turn(v_in, v_t, i)
+
+    each(1, arrive)
+    each(0, lambda i: send_out(i, dot(v_t[...], prob[:, block(i, wide)]) * inv_sum[i, 0:1, :]), EARLY)
+    hand_on(2)
+    hand_on(6)
+    lax.fori_loop(EARLY, n, late, 0)
 
     def prepare(i, carry):
         @pl.when(i > 0)
         def _():
             g_copy(i).wait_recv()
 
-        g = g_in[i].astype(F32).T
-        g_split = split_heads(g)
-        g_t[:, block(i, wide)] = g_split.astype(BF16)
-        g_l[block(i, wide), :] = (g_split * inv_sum[i, 0:1, :]).T.astype(BF16)
+        g = g_in[i].astype(F32)
+        g_t[:, block(i, wide)] = split_heads(g).astype(BF16)
+        g_l[block(i, wide), :] = scaled_rows(g.T, column(inv_sum[i, 0:1, :]))
         product = out_all[i] * g
         both = jnp.concatenate(
             [
@@ -384,63 +432,65 @@
         return carry
 
     lax.fori_loop(0, n, prepare, 0)
+    weight_part(1)
+    dq_t[...] = jnp.zeros_like(dq_t)
     share(1)
-    dq_t[...] = jnp.zeros_like(dq_t)
-
-    def backward(j, carry):
-        keys = block(j, rows)
-
-        def grad_chunk(i, carry):
+
+    def grad_q(i):
+        return merge_heads(dq_t[:, block(i, wide)] * (inv_sum[i, 0:1, :] * SCALING)).T.astype(BF16)
+
+    def backward(j, last):
+        keys = block(j, span)
+
+        def grad_chunk(i):
             cut = block(i, wide)
             grad_prob = dot(v_rows[keys, :], g_t[:, cut])
             grad_score = (prob[keys, cut].astype(F32) * (grad_prob - row_dot[i, 0:1, :])).astype(BF16)
             ds_buf[:, cut] = grad_score
             dq_t[:, cut] += dot(k_t[:, keys], grad_score)
-            return carry
-
-        lax.fori_loop(0, n, grad_chunk, 0, unroll=True)
+            if last:
+                dq_out[i] = grad_q(i)
+                if i:
+                    d_copy(0, i).start()
+
+        for i in range(n):
+            grad_chunk(i)
         grad_v = dot(prob[keys, :], g_l[...]).astype(BF16)
         grad_k = dot(ds_buf[...], q_l[...]).astype(BF16)
 
-        @pl.when(j == 0)
-        def _():
-            dqkv_ref[0, :, block(n + s, LANES)] = grad_k
-            dqkv_ref[0, :, block(2 * n + s, LANES)] = grad_v
-
-        @pl.when(j > 0)
-        def _():
-            dk_out[j] = grad_k
-            d_copy(1, j).start()
-            dv_out[j] = grad_v
-            d_copy(2, j).start()
-
-        @pl.when(j == n - 4)
+        for part in range(SPAN):
+            i = j * SPAN + part
+            cut = slice(part * rows, (part + 1) * rows)
+            dk_out[i] = grad_k[cut]
+            dv_out[i] = grad_v[cut]
+
+            @pl.when(i > 0)
+            def _():
+                d_copy(1, i).start()
+                d_copy(2, i).start()
+
+    def backward_step(j, carry):
+        backward(j, False)
+
+        @pl.when(j == steps - 3)
         def _():
             row_sum()
 
-        @pl.when(j == n - 2)
-        def _():
-            chip_sum()
+        @pl.when(j == steps - 2)
+        def _():
+            patch_sum()
 
         return carry
 
-    lax.fori_loop(0, n, backward, 0)
-
-    def grad_q(i):
-        return merge_heads(dq_t[:, block(i, wide)] * (inv_sum[i, 0:1, :] * SCALING)).T.astype(BF16)
-
-    def finish(i):
-        dq_out[i] = grad_q(i)
-        d_copy(0, i).start()
-
-    each(1, finish)
-    dqkv_ref[0, :, block(s, LANES)] = grad_q(0)
+    lax.fori_loop(0, steps - 1, backward_step, 0)
+    backward(steps - 1, True)
     weight_out()
+    for t in range(3):
+        dqkv_ref[0, :, block(t * n + s, LANES)] = (dq_out, dk_out, dv_out)[t][0]
 
     def arrivals(i):
         for t in range(3):
             d_copy(t, i).wait_recv()
-        gw_copy(i).wait_recv()
 
     each(1, arrivals)
 
@@ -450,8 +500,6 @@
             d_copy(t, i).wait_send()
         g_copy(i).wait_send()
         o_copy(i).wait_send()
-        gs_copy(i).wait_send()
-        gw_copy(i).wait_send()
 
     each(1, sent)
     for slot in range(n):
@@ -460,7 +508,11 @@
         ws_copy(slot).wait_send()
     sib_copy(0).wait_send()
     sib_copy(1).wait_send()
-    y_copy().wait_send()
+    for k in range(3):
+        ys_copy(k).wait_send()
+        zs_copy(k + 1).wait_send()
+        gw_copy(k + 1).wait_send()
+        gw_copy(k + 1).wait_recv()
 
     def rs_sent(i):
         @pl.when(where_to(i)[1] > 0)
@@ -484,15 +536,16 @@
     return pl.pallas_call(
         functools.partial(kernel, n, rows, width),
         out_shape=(
-            jax.ShapeDtypeStruct((1, rows, 3 * features), BF16),
-            jax.ShapeDtypeStruct((share_rows, width), F32),
+            vmem((1, rows, 3 * features), BF16),
+            vmem((share_rows, width), F32),
         ),
         in_specs=[pl.BlockSpec(memory_space=pl.ANY)] * 5,
         out_specs=[pl.BlockSpec(memory_space=vmem)] * 2,
         scratch_shapes=[
-            flat, flat, flat, flat,
+            flat, flat, flat, turned,
             vmem((n, LANES, width), BF16),
             vmem((rows, width), BF16),
+            vmem((width, rows), BF16),
             vmem((LANES, length), BF16),
             vmem((LANES, length), BF16),
             vmem((length, wide), F32),
@@ -505,24 +558,24 @@
             vmem((LANES, n * wide), BF16),
             vmem((n * wide, LANES), BF16),
             vmem((n * wide, LANES), BF16),
-            vmem((rows, n * wide), BF16),
+            vmem((SPAN * rows, n * wide), BF16),
             vmem((LANES, n * wide), F32),
-            flat, turned, turned,
+            turned, turned, turned,
             vmem((n * HEAD_DIM, rows), BF16),
             shares, shares, shares, shares, shares,
             vmem((2, HEAD_DIM, width), F32),
-            vmem((HEAD_DIM, width), BF16),
-            vmem((HEAD_DIM, width), BF16),
-            vmem((n, HEAD_DIM, columns), F32),
-            vmem((n, HEAD_DIM, columns), BF16),
-            vmem((n, HEAD_DIM, columns), BF16),
-            vmem((HEAD_DIM, columns), F32),
+            vmem((Z, 2, HEAD_DIM, width // Z), F32),
+            vmem((Z, 2, HEAD_DIM, width // Z), BF16),
+            vmem((Z, 2, HEAD_DIM, width // Z), BF16),
+            vmem((2, HEAD_DIM, width // Z), BF16),
+            vmem((4, HEAD_DIM, width // Z), BF16),
+            vmem((HEAD_DIM, width // Z), F32),
             flat, flat, flat,
             dma((3, n)), dma((3, n)),
             dma((n,)), dma((n,)), dma((n,)), dma((n,)),
             dma((n,)), dma((n,)), dma((n,)), dma((n,)),
-            dma((2,)), dma((2,)), dma((n,)), dma((n,)), dma((1,)), dma((1,)),
-            dma((n,)), dma((n,)), dma((n,)), dma((n,)),
+            dma((2,)), dma((2,)), dma((n,)), dma((n,)),
+            dma((Z,)), dma((Z,)), dma((3,)), dma((3,)), dma((Z,)), dma((Z,)),
             dma((3, n)), dma((3, n)), dma((5,)),
         ],
         compiler_params=pltpu.CompilerParams(

time: 120 us -> 115 us (0.958)
  Pallas kernels: 116 us -> 112 us
  local copies, waits for them, and re-layouts: 3.51 us -> 1.94 us
    pallas_call x1, Pallas kernels: 116 us -> 112 us  [on_device(): pl.pallas_call(functools.partial(kernel, n, rows, width), out_shape=(vmem...]
    unnamed x4 -> x2, local copies, waits for them, and re-layouts: 3.51 us -> 1.94 us
where the time goes in v4:
time: 115 us
  Pallas kernels  112 us (97%)
  local copies, waits for them, and re-layouts  1.94 us (2%)
    pallas_call x1, Pallas kernels, on_device(): pl.pallas_call(functools.partial(kernel, n, rows, width), out_shape=(vmem...  112 us

profile of v4, /device:TPU:1, one launch (start us, length us, event | category | flops | bytes accessed | tf_op | source)
XLA Modules:
  0.0 115.0 jit_solution(13483913560989216119)
XLA Ops:
  0.6 112.4 %shard_map.68 = (bf16[1,256,3072]{2,1,0:T(8,128)(2,1)S(1)}, f32[64,2048]{1,0:T(8,128)S(1)}) custom-call(bf16[1,256,1024]{2,1,0:T(8,128)(2,1)} %q_ref.1, bf16[1,256,1024]{2,1,0:T(8,128)(2,1)} %k_ref.1, bf16[1,256,1024]{2,1,0:T(8,128)(2,1)} %v_ref.1, bf16[64,2048]{1,0:T(8,128)(2,1)} %w_ref.1, bf16[1,256,2048]{2,1,0:T(8,128)(2,1)} %go_ref.1), custom_call_target="tpu_custom_call" | custom-call | tf_op jit(solution)/shard_map/pallas_call | solution.py:536
  113.0 1.1 copy.9
  114.2 0.8 copy.10

commit v5 on v4

--- a/solution.py
+++ b/solution.py
@@ -50,7 +50,7 @@
     q_in, k_in, v_in, g_in, w_all, go, go_t, k_t, v_t,
     score, prob, q_t, out_t, inv_sum, out_all, row_dot, g_t, g_l, q_l, ds_buf, dq_t,
     g_out, o_out, o_in, o_rows, own_part, sib_out, sib_in, rs_out, rs_in, home,
-    total, zs_out, zs_in, ys_out, ys_in, done, dq_out, dk_out, dv_out,
+    total, zs_out, zs_in, ys_out, ys_in, done, gw_in, dq_out, dk_out, dv_out,
     qkv_send, qkv_recv, w_send, w_recv, ws_send, ws_recv, g_send, g_recv, o_send, o_recv,
     sib_send, sib_recv, rs_send, rs_recv, zs_send, zs_recv, ys_send, ys_recv, gw_send, gw_recv,
     d_send, d_recv, local_sem,
@@ -152,7 +152,7 @@
     def gw_copy(k):
         to = lax.rem(z + k, Z)
         return remote(
-            done, gw_ref.at[:, block(z, quarter)], gw_send.at[k], gw_recv.at[k], {"seq": 2 * to + y_hi}
+            done, gw_in.at[k], gw_send.at[k], gw_recv.at[k], {"seq": 2 * to + y_hi}
         )
 
     def d_copy(t, i):
@@ -297,10 +297,10 @@
         value = ys_in[0].astype(F32)
         for at in range(1, 4):
             value += ys_in[at].astype(F32)
-        done[...] = value
+        done[...] = value.astype(BF16)
         for k in range(1, Z):
             gw_copy(k).start()
-        gw_ref[:, block(z, quarter)] = value
+        gw_ref[:, block(z, quarter)] = done[...].astype(F32)
 
     def column(value):
         return jnp.broadcast_to(value, (8, wide)).T[:, 0:1]
@@ -513,6 +513,7 @@
         zs_copy(k + 1).wait_send()
         gw_copy(k + 1).wait_send()
         gw_copy(k + 1).wait_recv()
+        gw_ref[:, block(lax.rem(z + Z - k - 1, Z), quarter)] = gw_in[k + 1].astype(F32)
 
     def rs_sent(i):
         @pl.when(where_to(i)[1] > 0)
@@ -569,7 +570,8 @@
             vmem((Z, 2, HEAD_DIM, width // Z), BF16),
             vmem((2, HEAD_DIM, width // Z), BF16),
             vmem((4, HEAD_DIM, width // Z), BF16),
-            vmem((HEAD_DIM, width // Z), F32),
+            vmem((HEAD_DIM, width // Z), BF16),
+            vmem((Z, HEAD_DIM, width // Z), BF16),
             flat, flat, flat,
             dma((3, n)), dma((3, n)),
             dma((n,)), dma((n,)), dma((n,)), dma((n,)),

time: 115 us -> 112 us (0.974)
  Pallas kernels: 112 us -> 110 us
    pallas_call x1, Pallas kernels: 112 us -> 110 us  [on_device(): pl.pallas_call(functools.partial(kernel, n, rows, width), out_shape=(vmem...]
where the time goes in v5:
time: 112 us
  Pallas kernels  110 us (98%)
  local copies, waits for them, and re-layouts  1.94 us (2%)
    pallas_call x1, Pallas kernels, on_device(): pl.pallas_call(functools.partial(kernel, n, rows, width), out_shape=(vmem...  110 us

profile of v5, /device:TPU:1, one launch (start us, length us, event | category | flops | bytes accessed | tf_op | source)
XLA Modules:
  0.0 112.2 jit_solution(10433930348130830454)
XLA Ops:
  0.6 109.7 %shard_map.68 = (bf16[1,256,3072]{2,1,0:T(8,128)(2,1)S(1)}, f32[64,2048]{1,0:T(8,128)S(1)}) custom-call(bf16[1,256,1024]{2,1,0:T(8,128)(2,1)} %q_ref.1, bf16[1,256,1024]{2,1,0:T(8,128)(2,1)} %k_ref.1, bf16[1,256,1024]{2,1,0:T(8,128)(2,1)} %v_ref.1, bf16[64,2048]{1,0:T(8,128)(2,1)} %w_ref.1, bf16[1,256,2048]{2,1,0:T(8,128)(2,1)} %go_ref.1), custom_call_target="tpu_custom_call" | custom-call | tf_op jit(solution)/shard_map/pallas_call | solution.py:537
  110.3 1.1 %copy.9 = bf16[1,256,3072]{2,1,0:T(8,128)(2,1)} copy(bf16[1,256,3072]{2,1,0:T(8,128)(2,1)S(1)} %get-tuple-element.2) | data formatting | bytes 3145728
  111.4 0.8 copy.10

commit v6 on v5

--- a/solution.py
+++ b/solution.py
@@ -13,7 +13,7 @@
 X = 4
 Z = 4
 SPAN = 2
-EARLY = 4
+EARLY = 2
 CHUNK = 512
 SCALING = HEAD_DIM ** (-0.5)
 EXP_SCALE = SCALING * math.log2(math.e)
@@ -373,10 +373,6 @@
             hand_on(5, 6)
             grad_attn(3, 1)
 
-        @pl.when(i == 2)
-        def _():
-            hand_on(7)
-
         return carry
 
     def late(i, carry):
@@ -386,17 +382,18 @@
         def _():
             grad_attn(2, 6)
 
-        @pl.when(i == batch + 1)
+        @pl.when(i == batch + 2)
         def _():
             weight_part(0)
 
-        @pl.when(i == batch + 2)
+        @pl.when(i == batch + 3)
         def _():
             share(0)
 
         return carry
 
     lax.fori_loop(0, EARLY, early, 0)
+    hand_on(7)
     turn(k_in, k_t, 0)
     each(1, lambda i: turn(k_in, k_t, i))
     grad_attn(5, 7)

time: 112 us -> 110 us (0.982)
  the two profiles are of different devices: /device:TPU:1 before, /device:TPU:2 now
where the time goes in v6:
time: 110 us
  Pallas kernels  108 us (98%)
  local copies, waits for them, and re-layouts  1.94 us (2%)
    pallas_call x1, Pallas kernels, on_device(): pl.pallas_call(functools.partial(kernel, n, rows, width), out_shape=(vmem...  108 us

profile of v6, /device:TPU:2, one launch (start us, length us, event | category | flops | bytes accessed | tf_op | source)
XLA Modules:
  0.0 110.3 jit_solution(470031698731158487)
XLA Ops:
  0.6 107.7 %shard_map.68 = (bf16[1,256,3072]{2,1,0:T(8,128)(2,1)S(1)}, f32[64,2048]{1,0:T(8,128)S(1)}) custom-call(bf16[1,256,1024]{2,1,0:T(8,128)(2,1)} %q_ref.1, bf16[1,256,1024]{2,1,0:T(8,128)(2,1)} %k_ref.1, bf16[1,256,1024]{2,1,0:T(8,128)(2,1)} %v_ref.1, bf16[64,2048]{1,0:T(8,128)(2,1)} %w_ref.1, bf16[1,256,2048]{2,1,0:T(8,128)(2,1)} %go_ref.1), custom_call_target="tpu_custom_call" | custom-call | tf_op jit(solution)/shard_map/pallas_call | solution.py:534
  108.4 1.1 %copy.9 = bf16[1,256,3072]{2,1,0:T(8,128)(2,1)} copy(bf16[1,256,3072]{2,1,0:T(8,128)(2,1)S(1)} %get-tuple-element.2) | data formatting | bytes 3145728
  109.5 0.8 copy.10

commit v7 on v6

--- a/solution.py
+++ b/solution.py
@@ -378,7 +378,12 @@
     def late(i, carry):
         probs(i, True)
 
-        @pl.when(i == EARLY)
+        @pl.when(i == EARLY + 1)
+        def _():
+            hand_on(2)
+            hand_on(6)
+
+        @pl.when(i == EARLY + 2)
         def _():
             grad_attn(2, 6)
 
@@ -405,8 +410,6 @@
 
     each(1, arrive)
     each(0, lambda i: send_out(i, dot(v_t[...], prob[:, block(i, wide)]) * inv_sum[i, 0:1, :]), EARLY)
-    hand_on(2)
-    hand_on(6)
     lax.fori_loop(EARLY, n, late, 0)
 
     def prepare(i, carry):

time: 110 us -> 110 us (level)
  the two profiles are of different devices: /device:TPU:2 before, /device:TPU:72 now
where the time goes in v7:
time: 110 us
  Pallas kernels  107 us (97%)
  local copies, waits for them, and re-layouts  1.94 us (2%)
    pallas_call x1, Pallas kernels, on_device(): pl.pallas_call(functools.partial(kernel, n, rows, width), out_shape=(vmem...  107 us

profile of v7, /device:TPU:72, one launch (start us, length us, event | category | flops | bytes accessed | tf_op | source)
XLA Modules:
  0.0 110.0 jit_solution(3147763285461699295)
XLA Ops:
  0.6 107.4 %shard_map.68 = (bf16[1,256,3072]{2,1,0:T(8,128)(2,1)S(1)}, f32[64,2048]{1,0:T(8,128)S(1)}) custom-call(bf16[1,256,1024]{2,1,0:T(8,128)(2,1)} %q_ref.1, bf16[1,256,1024]{2,1,0:T(8,128)(2,1)} %k_ref.1, bf16[1,256,1024]{2,1,0:T(8,128)(2,1)} %v_ref.1, bf16[64,2048]{1,0:T(8,128)(2,1)} %w_ref.1, bf16[1,256,2048]{2,1,0:T(8,128)(2,1)} %go_ref.1), custom_call_target="tpu_custom_call" | custom-call | tf_op jit(solution)/shard_map/pallas_call | solution.py:537
  108.0 1.1 %copy.9 = bf16[1,256,3072]{2,1,0:T(8,128)(2,1)} copy(bf16[1,256,3072]{2,1,0:T(8,128)(2,1)S(1)} %get-tuple-element.2) | data formatting | bytes 3145728
  109.2 0.8 copy.10
